TPU v7x, 128 devices: a whole 4x4x4 slice. The times are simulated.
128 devices in a mesh: dom: 8 (over y_hi, z), blk: 16 (over y_lo, x, core).
Axes of the slice: x: 4, y: 4 (y_hi: 2, y_lo: 2; y = y_hi * 2 + y_lo), z: 4, core: 2. Of those that a mesh axis runs over, the one named last changes fastest.
Arguments:
- features_domain: bfloat16 [98304, 1152], P(('dom', 'blk')), may hold values from -6 to 6
- arrival: int32 [98304], P(('dom', 'blk')), may hold values from 0 to 767, as said below
- positions: float32 [98304, 3], P(('dom', 'blk')), may hold values from 0 to 3072, as said below
- species: int32 [98304], P(('dom', 'blk')), may hold values from 0 to 88
- block_count: int32 [1536], P(('dom', 'blk')), may hold values from 16 to 64, as said below
- pair_block: int32 [1536, 3], P(('dom', 'blk')), may hold values from -1 to 1535, as said below
- radial_weights: float32 [8, 7, 128], replicated, may hold values from -0.75 to 0.75
- species_weights: float32 [89, 3, 128], replicated, may hold values from -1 to 1
- mix_weight: bfloat16 [128, 128], replicated, may hold values from -0.5 to 0.5
- self_weight: bfloat16 [128, 128], replicated, may hold values from -0.5 to 0.5
- readout: float32 [128], replicated, may hold values from -0.5 to 0.5
Outputs:
- atom_energy: float32 [98304], P(('dom', 'blk'))
- forces: float32 [98304, 3], P(('dom', 'blk'))
- new_features: bfloat16 [98304, 128], P(('dom', 'blk'))
Inputs may be any that keep to these rules, and one draw needn't show every extreme that they name: `arrival`: on each device of dom+blk its 768 entries are a permutation of 0 to 767. `pair_block`: entry [b, 0] is b - 1 or -1, entry [b, 1] is b, entry [b, 2] is b + 1 or -1; the lists are symmetric: [b, 2] is b + 1 exactly when [b + 1, 0] is b. The first block has no predecessor and the last no successor. `block_count`: the live atoms of a block are its first slots. `positions`: atoms of blocks that are not paired lie a distance of 1 or more apart.
All inputs are finite; a program needn't handle non-finite values.
Results may differ from a plain program's by a relative error of at most 0.015.
Values may be sent and summed in bfloat16 or wider, within the bound.
A program may use at most 64 MiB of HBM per device.

v0:
```python
import math

import jax
import jax.numpy as jnp
import numpy as np
from jax import lax
from jax.sharding import PartitionSpec as P

BLOCK = 64


ROOT_THREE = math.sqrt(3.0)
DOT_PATH = np.array([0, 5, 5, 5, 6, 6, 6, 6, 6])
CARRY_PATH = np.array([3, 3, 3, 4, 4, 4, 4, 4])


def extended(block, sides, width):
    for axis, dim in sides:
        count = lax.axis_size(axis)
        forward = [(i, i + 1) for i in range(count - 1)]
        backward = [(target, source) for source, target in forward]
        low = lax.ppermute(
            lax.slice_in_dim(block, block.shape[dim] - width, None, axis=dim), axis, forward
        )
        high = lax.ppermute(lax.slice_in_dim(block, 0, width, axis=dim), axis, backward)
        block = jnp.concatenate([low, block, high], axis=dim)
    return block


def harmonics(delta_x, delta_y, delta_z):
    return jnp.stack(
        [
            jnp.ones_like(delta_x),
            delta_x,
            delta_y,
            delta_z,
            ROOT_THREE * delta_x * delta_y,
            ROOT_THREE * delta_y * delta_z,
            0.5 * (2.0 * delta_z * delta_z - delta_x * delta_x - delta_y * delta_y),
            ROOT_THREE * delta_z * delta_x,
            0.5 * ROOT_THREE * (delta_x * delta_x - delta_y * delta_y),
        ]
    )


def pair_mask(pair_row, block_rows):
    columns = jnp.arange(3 * block_rows, dtype=jnp.int32)
    listed = (pair_row >= 0).astype(jnp.float32)
    slot_mask = jnp.where(
        columns < block_rows, listed[0], jnp.where(columns < 2 * block_rows, listed[1], listed[2])
    )
    targets = jnp.arange(block_rows, dtype=jnp.int32)[:, None] + block_rows
    distinct = (targets != columns[None, :]).astype(jnp.float32)
    return slot_mask[None, :] * distinct


def edge_factors(window_pos, pair_keep, basis_count):
    block_rows = pair_keep.shape[0]
    coords = window_pos.T
    centre = coords[:, block_rows : 2 * block_rows]
    delta_x = coords[0][None, :] - centre[0][:, None]
    delta_y = coords[1][None, :] - centre[1][:, None]
    delta_z = coords[2][None, :] - centre[2][:, None]
    spread = delta_x * delta_x + delta_y * delta_y + delta_z * delta_z
    envelope = jnp.maximum(1.0 - spread, 0.0) ** 3 * pair_keep
    orders = jnp.arange(basis_count, dtype=jnp.float32) * math.pi
    radial = envelope[None] * jnp.cos(orders[:, None, None] * spread[None])
    return (radial[:, None] * harmonics(delta_x, delta_y, delta_z)[None]).astype(jnp.bfloat16)


def feature_terms(window_feat, radial_weights):
    values = window_feat.astype(jnp.float32)
    dot_terms = (radial_weights[:, None, DOT_PATH, :] * values[None]).astype(jnp.bfloat16)
    lift_terms = (radial_weights[:, None, 1:3, :] * values[None, :, 0:1, :]).astype(jnp.bfloat16)
    carry_terms = (radial_weights[:, None, CARRY_PATH, :] * values[None, :, 1:, :]).astype(
        jnp.bfloat16
    )
    return (dot_terms, lift_terms, carry_terms)


def block_messages(edges, dot_terms, lift_terms, carry_terms):
    scalar = jnp.einsum("nyij,njyc->ic", edges, dot_terms, preferred_element_type=jnp.float32)
    first_order = jnp.einsum(
        "nmij,njc->mic", edges[:, 1:4], lift_terms[:, :, 0], preferred_element_type=jnp.float32
    )
    second = jnp.einsum(
        "nmij,njc->mic", edges[:, 4:9], lift_terms[:, :, 1], preferred_element_type=jnp.float32
    )
    carried = jnp.einsum(
        "nij,njyc->yic", edges[:, 0], carry_terms, preferred_element_type=jnp.float32
    )
    return jnp.concatenate(
        [scalar[None], first_order + carried[0:3], second + carried[3:8]], axis=0
    )


def atom_outputs(message_rows, gain_rows, self_part, live_rows, mix_weight, self_weight, readout):
    squares = message_rows * message_rows
    basis_rows = (
        message_rows[0]
        + gain_rows[:, 0] * squares[0]
        + gain_rows[:, 1] * jnp.sum(squares[1:4], axis=0)
        + gain_rows[:, 2] * jnp.sum(squares[4:9], axis=0)
    )
    rounded = basis_rows.astype(jnp.bfloat16)
    mixed_rows = jnp.dot(rounded, mix_weight, preferred_element_type=jnp.float32) + jnp.dot(
        self_part, self_weight, preferred_element_type=jnp.float32
    )
    energy = live_rows * jnp.sum(readout[None, :] * jax.nn.silu(mixed_rows), axis=1)
    return (energy, (mixed_rows * live_rows[:, None]).astype(jnp.bfloat16))


def block_outputs(
    window_pos,
    window_feat,
    pair_row,
    gain_rows,
    live_rows,
    radial_weights,
    mix_weight,
    self_weight,
    readout,
):
    block_rows = gain_rows.shape[0]
    pair_keep = pair_mask(pair_row, block_rows)
    dot_terms, lift_terms, carry_terms = feature_terms(window_feat, radial_weights)

    def messages_of(positions_window):
        edges = edge_factors(positions_window, pair_keep, radial_weights.shape[0])
        return block_messages(edges, dot_terms, lift_terms, carry_terms)

    messages, pull_edges = jax.vjp(messages_of, window_pos)
    self_rows = window_feat[block_rows : 2 * block_rows, 0, :]

    def outputs_of(message_rows):
        return atom_outputs(
            message_rows, gain_rows, self_rows, live_rows, mix_weight, self_weight, readout
        )

    energy, pull_atoms, features_out = jax.vjp(outputs_of, messages, has_aux=True)
    (grad_messages,) = pull_atoms(jnp.ones_like(energy))
    (grad_window,) = pull_edges(grad_messages)
    return (energy, features_out, grad_window)


def per_device(
    features_domain,
    arrival,
    positions,
    species,
    block_count,
    pair_block,
    radial_weights,
    species_weights,
    mix_weight,
    self_weight,
    readout,
):
    devices = lax.axis_size(("dom", "blk"))
    atom_rows, feature_cols = features_domain.shape
    piece_rows = atom_rows // devices
    parcels = features_domain.reshape(devices, piece_rows, feature_cols)
    received = lax.all_to_all(parcels, ("dom", "blk"), split_axis=0, concat_axis=0, tiled=True)
    received = received.reshape(atom_rows, feature_cols)
    slot_index = jnp.arange(atom_rows, dtype=jnp.int32)
    live_slots = slot_index % BLOCK < jnp.repeat(block_count, BLOCK, total_repeat_length=atom_rows)
    relaid = jnp.where(
        live_slots[:, None], jnp.take(received, arrival, axis=0), jnp.zeros((), jnp.bfloat16)
    )
    live_float = live_slots.astype(jnp.float32)
    feature_ext = extended(relaid, ((("dom", "blk"), 0),), BLOCK)
    position_ext = extended(positions, ((("dom", "blk"), 0),), BLOCK)
    feature_view = feature_ext.reshape(atom_rows + 2 * BLOCK, 9, -1)
    species_total = species_weights.shape[0]
    one_hot = (species[:, None] == jnp.arange(species_total, dtype=jnp.int32)[None, :]).astype(
        jnp.float32
    )
    gains = jnp.dot(
        one_hot, species_weights.reshape(species_total, -1), precision=lax.Precision.HIGHEST
    ).reshape(atom_rows, 3, -1)
    channels = radial_weights.shape[2]

    def one_block(block_index, loop_state):
        force_ext, energies, new_rows = loop_state
        start_row = block_index * BLOCK
        window_pos = lax.dynamic_slice_in_dim(position_ext, start_row, 3 * BLOCK, 0)
        window_feat = lax.dynamic_slice_in_dim(feature_view, start_row, 3 * BLOCK, 0)
        pair_row = lax.dynamic_index_in_dim(pair_block, block_index, 0, keepdims=False)
        gain_rows = lax.dynamic_slice_in_dim(gains, start_row, BLOCK, 0)
        live_rows = lax.dynamic_slice_in_dim(live_float, start_row, BLOCK, 0)
        energy, features_out, grad_window = block_outputs(
            window_pos,
            window_feat,
            pair_row,
            gain_rows,
            live_rows,
            radial_weights,
            mix_weight,
            self_weight,
            readout,
        )
        current = lax.dynamic_slice_in_dim(force_ext, start_row, 3 * BLOCK, 0)
        force_ext = lax.dynamic_update_slice_in_dim(force_ext, current + grad_window, start_row, 0)
        energies = lax.dynamic_update_slice_in_dim(energies, energy, start_row, 0)
        new_rows = lax.dynamic_update_slice_in_dim(new_rows, features_out, start_row, 0)
        return (force_ext, energies, new_rows)

    initial = (
        jnp.zeros((atom_rows + 2 * BLOCK, 3), jnp.float32),
        jnp.zeros((atom_rows,), jnp.float32),
        jnp.zeros((atom_rows, channels), jnp.bfloat16),
    )
    force_ext, energies, new_rows = lax.fori_loop(0, atom_rows // BLOCK, one_block, initial)
    outgoing = jnp.concatenate([force_ext[:BLOCK], force_ext[atom_rows + BLOCK :]], axis=0)
    incoming = extended(outgoing, ((("dom", "blk"), 0),), BLOCK)
    own_forces = force_ext[BLOCK : atom_rows + BLOCK]
    own_forces = own_forces.at[:BLOCK].add(incoming[:BLOCK])
    own_forces = own_forces.at[atom_rows - BLOCK :].add(incoming[3 * BLOCK :])
    return (energies, -own_forces, new_rows)


def solution(mesh):
    placed = (
        P(("dom", "blk"), None),
        P(("dom", "blk")),
        P(("dom", "blk"), None),
        P(("dom", "blk")),
        P(("dom", "blk")),
        P(("dom", "blk"), None),
        P(),
        P(),
        P(),
        P(),
        P(),
    )
    return jax.shard_map(
        per_device,
        mesh=mesh,
        in_specs=placed,
        out_specs=(P(("dom", "blk")), P(("dom", "blk"), None), P(("dom", "blk"), None)),
        check_vma=False,
    )
```

profile of v0, /device:TPU:111, one launch (start us, length us, event | category | flops | bytes accessed | tf_op | source)
XLA Modules:
  0.0 521.6 jit_solution(16700686446321049419)
XLA Ops:
  0.6 3.9 reshape.1382
  4.6 10.5 %all-to-all-start = ((bf16[128,6,1152]{2,1,0:T(8,128)(2,1)}), bf16[128,6,1152]{2,1,0:T(8,128)(2,1)}, u32[]{:S(2)}, u32[]{:S(2)}) async-start(bf16[128,6,1152]{2,1,0:T(8,128)(2,1)} %reshape.1382), calls=%async_computation | async-start | bytes 4718592 | tf_op jit(solution)/shard_map/all_to_all | solution.py:163
  15.7 2.6 collective-permute-start
  18.3 1.9 collective-permute-start.1
  21.9 4.3 fusion.111
  26.9 3.8 fusion.115
  30.7 11.7 %all-to-all-done = bf16[128,6,1152]{2,1,0:T(8,128)(2,1)} async-done(((bf16[128,6,1152]{2,1,0:T(8,128)(2,1)}), bf16[128,6,1152]{2,1,0:T(8,128)(2,1)}, u32[]{:S(2)}, u32[]{:S(2)}) %all-to-all-start) | async-done | bytes 1769504 | tf_op jit(solution)/shard_map/all_to_all | solution.py:163
  42.4 2.7 reshape.1383
  45.1 2.9 gather_fusion.2
  49.2 6.4 %collective-permute-start.2 = (bf16[64,1152]{1,0:T(8,128)(2,1)S(1)}, bf16[64,1152]{1,0:T(8,128)(2,1)S(1)}, u32[]{:S(2)}, u32[]{:S(2)}) collective-permute-start(bf16[64,1152]{1,0:T(8,128)(2,1)S(1)} %get-tuple-element.459), channel_id=1, source_target_pairs={{0,1},{1,2},{2,3},{3,4},{4,5},{5,6},{6,7},{7,8},{8,9},{9,10},{10,1... | collective-permute-start | bytes 442376 | tf_op jit(solution)/shard_map/ppermute | solution.py:22
  55.6 2.1 collective-permute-start.3
  60.2 6.1 %collective-permute-done.3 = bf16[64,1152]{1,0:T(8,128)(2,1)S(1)} collective-permute-done((bf16[64,1152]{1,0:T(8,128)(2,1)S(1)}, bf16[64,1152]{1,0:T(8,128)(2,1)S(1)}, u32[]{:S(2)}, u32[]{:S(2)}) %collective-permute-start.3) | collective-permute-done | bytes 147488 | tf_op jit(solution)/shard_map/ppermute | solution.py:25
  67.8 2.9 copy.29
  70.7 2.4 copy.32
  75.0 433.1 %while.21 = (s32[]{:T(128)}, f32[896,3]{0,1:T(4,128)}, f32[768]{0:T(1024)}, bf16[768,128]{1,0:T(8,128)(2,1)}, f32[896,3]{0,1:T(4,128)S(1)}, /*index=5*/s32[12,3]...) while((s32[]{:T(128)}, f32[896,3]{0,1:T(4,128)}, ...), condition=%wide.region_14.15_spmd.clone, body=%wide.region_0.14_spmd.sunk.clone.sunk | while | flops 1296982656 | bytes 45422888 | solution.py:213
  76.7 1.9 compare_select_fusion.13
  85.1 1.9 fusion.179
  103.0 3.0 fusion.190
  106.0 2.2 fusion.191
  112.8 1.9 compare_select_fusion.13
  121.1 1.9 fusion.179
  139.0 3.0 fusion.190
  142.1 2.2 fusion.191
  149.0 1.9 compare_select_fusion.13
  157.3 1.9 fusion.179
  175.2 3.0 fusion.190
  178.2 2.2 fusion.191
  185.0 1.9 compare_select_fusion.13
  193.4 1.9 fusion.179
  211.2 3.0 fusion.190
  214.3 2.2 fusion.191
  221.2 1.9 compare_select_fusion.13
  229.5 1.9 fusion.179
  247.4 3.0 fusion.190
  250.5 2.2 fusion.191
  257.2 1.9 compare_select_fusion.13
  265.6 1.9 fusion.179
  283.5 3.0 fusion.190
  286.5 2.2 fusion.191
  293.4 1.9 compare_select_fusion.13
  301.8 1.9 fusion.179
  319.6 3.0 fusion.190
  322.7 2.2 fusion.191
  337.8 1.9 fusion.179
  355.7 3.0 fusion.190
  358.7 2.2 fusion.191
  374.0 1.9 fusion.179
  391.8 3.0 fusion.190
  394.9 2.2 fusion.191
  401.6 1.9 compare_select_fusion.13
  410.0 1.9 fusion.179
  427.9 3.0 fusion.190
  430.9 2.2 fusion.191
  437.8 1.9 compare_select_fusion.13
  446.2 1.9 fusion.179
  464.0 3.0 fusion.190
  467.1 2.2 fusion.191
  473.8 1.9 compare_select_fusion.13
  482.2 1.9 fusion.179
  500.0 3.0 fusion.190
  503.1 2.2 fusion.191
  508.9 1.9 collective-permute-start.4
  511.6 2.4 collective-permute-start.5
  514.9 5.9 %collective-permute-done.5 = f32[64,3]{0,1:T(4,128)S(1)} collective-permute-done((f32[64,3]{0,1:T(4,128)S(1)}, f32[64,3]{0,1:T(4,128)S(1)}, u32[]{:S(2)}, u32[]{:S(2)}) %collective-permute-start.5) | collective-permute-done | bytes 800 | tf_op jit(solution)/shard_map/ppermute | solution.py:25
  (1459 shorter events, 334.2 us)
Async XLA Ops:
  4.5 10.5 %copy-start.32 = (f32[768,3]{0,1:T(4,128)S(1)}, f32[768,3]{0,1:T(4,128)}, u32[]{:S(2)}) copy-start(f32[768,3]{0,1:T(4,128)} %param.25) | copy-start | bytes 27652
  4.5 15.7 %copy-start.22 = (f32[89,3,128]{2,0,1:T(8,128)S(1)}, f32[89,3,128]{2,0,1:T(8,128)}, u32[]{:S(2)}) copy-start(f32[89,3,128]{2,0,1:T(8,128)} %param.30) | copy-start | bytes 410116
  4.5 16.6 %copy-start.33 = (s32[768]{0:T(1024)S(1)}, s32[768]{0:T(1024)}, u32[]{:S(2)}) copy-start(s32[768]{0:T(1024)} %param.24) | copy-start | bytes 9220
  4.5 16.6 %copy-start.27 = (s32[12]{0:T(128)S(1)}, s32[12]{0:T(128)}, u32[]{:S(2)}) copy-start(s32[12]{0:T(128)} %param.27) | copy-start | bytes 148
  4.5 17.3 %copy-start.34 = (s32[6,128]{1,0:T(8,128)S(1)}, s32[6,128]{1,0:T(8,128)}, u32[]{:S(2)}) copy-start(s32[6,128]{1,0:T(8,128)} %constant.303.clone.1) | copy-start | bytes 9220
  4.6 37.9 %all-to-all-start = ((bf16[128,6,1152]{2,1,0:T(8,128)(2,1)}), bf16[128,6,1152]{2,1,0:T(8,128)(2,1)}, u32[]{:S(2)}, u32[]{:S(2)}) async-start(bf16[128,6,1152]{2,1,0:T(8,128)(2,1)} %reshape.1382), calls=%async_computation | async-start | bytes 4718592 | tf_op jit(solution)/shard_map/all_to_all | solution.py:163
  15.7 43.7 %collective-permute-start = (f32[64,3]{0,1:T(4,128)}, f32[64,3]{0,1:T(4,128)}, u32[]{:S(2)}, u32[]{:S(2)}) collective-permute-start(f32[64,3]{0,1:T(4,128)} %get-tuple-element.463), channel_id=1, source_target_pairs={{0,1},{1,2},{2,3},{3,4},{4,5},{5,6},{6,7},{7,8},{8,9},{9,10},{10,1... | collective-permute-start | bytes 2312 | tf_op jit(solution)/shard_map/ppermute | solution.py:22
  18.3 41.2 %collective-permute-start.1 = (f32[64,3]{0,1:T(4,128)}, f32[64,3]{0,1:T(4,128)}, u32[]{:S(2)}, u32[]{:S(2)}) collective-permute-start(f32[64,3]{0,1:T(4,128)} %get-tuple-element.464), channel_id=1, source_target_pairs={{1,0},{2,1},{3,2},{4,3},{5,4},{6,5},{7,6},{8,7},{9,8},{10,9},{11,1... | collective-permute-start | bytes 2312 | tf_op jit(solution)/shard_map/ppermute | solution.py:25
  48.0 9.7 %copy-start.19 = (f32[3,128,89]{1,0,2:T(4,128)S(1)}, f32[3,128,89]{1,0,2:T(4,128)}, u32[]{:S(2)}) copy-start(f32[3,128,89]{1,0,2:T(4,128)} %dot_general.85) | copy-start | bytes 410116
  48.0 9.7 %copy-start.39 = (s32[768]{0:T(1024)S(1)}, s32[768]{0:T(1024)}, u32[]{:S(2)}) copy-start(s32[768]{0:T(1024)} %param.26) | copy-start | bytes 9220
  49.2 11.0 %collective-permute-start.2 = (bf16[64,1152]{1,0:T(8,128)(2,1)S(1)}, bf16[64,1152]{1,0:T(8,128)(2,1)S(1)}, u32[]{:S(2)}, u32[]{:S(2)}) collective-permute-start(bf16[64,1152]{1,0:T(8,128)(2,1)S(1)} %get-tuple-element.459), channel_id=1, source_target_pairs={{0,1},{1,2},{2,3},{3,4},{4,5},{5,6},{6,7},{7,8},{8,9},{9,10},{10,1... | collective-permute-start | bytes 442376 | tf_op jit(solution)/shard_map/ppermute | solution.py:22
  55.6 10.7 %collective-permute-start.3 = (bf16[64,1152]{1,0:T(8,128)(2,1)S(1)}, bf16[64,1152]{1,0:T(8,128)(2,1)S(1)}, u32[]{:S(2)}, u32[]{:S(2)}) collective-permute-start(bf16[64,1152]{1,0:T(8,128)(2,1)S(1)} %get-tuple-element.460), channel_id=1, source_target_pairs={{1,0},{2,1},{3,2},{4,3},{5,4},{6,5},{7,6},{8,7},{9,8},{10,9},{11,1... | collective-permute-start | bytes 442376 | tf_op jit(solution)/shard_map/ppermute | solution.py:25
  91.3 9.5 %copy-start.3 = (f32[192,8,128]{2,0,1:T(8,128)S(1)}, f32[192,8,128]{2,0,1:T(8,128)}, u32[]{:S(2)}) copy-start(f32[192,8,128]{2,0,1:T(8,128)} %slice.481) | copy-start | bytes 2359300 | tf_op jit(solution)/shard_map/while
  102.9 8.2 %copy-start.26 = (f32[896,3]{0,1:T(4,128)S(1)}, f32[896,3]{0,1:T(4,128)}, u32[]{:S(2)}) copy-start(f32[896,3]{0,1:T(4,128)} %copy-done.25) | copy-start | bytes 32260 | tf_op jit(solution)/shard_map/while
  102.9 8.2 %copy-start.29 = (s32[12,3]{0,1:T(4,128)S(1)}, s32[12,3]{0,1:T(4,128)}, u32[]{:S(2)}) copy-start(s32[12,3]{0,1:T(4,128)} %get-tuple-element.718) | copy-start | bytes 436 | tf_op jit(solution)/shard_map/while
  102.9 8.1 %copy-start.36 = (s32[8]{0:T(128)S(1)}, s32[8]{0:T(128)}, u32[]{:S(2)}) copy-start(s32[8]{0:T(128)} %get-tuple-element.743) | copy-start | bytes 100 | tf_op jit(solution)/shard_map/while
  103.0 8.1 %copy-start.38 = (s32[9]{0:T(128)S(1)}, s32[9]{0:T(128)}, u32[]{:S(2)}) copy-start(s32[9]{0:T(128)} %get-tuple-element.769) | copy-start | bytes 112 | tf_op jit(solution)/shard_map/while
  127.4 9.5 %copy-start.3 = (f32[192,8,128]{2,0,1:T(8,128)S(1)}, f32[192,8,128]{2,0,1:T(8,128)}, u32[]{:S(2)}) copy-start(f32[192,8,128]{2,0,1:T(8,128)} %slice.481) | copy-start | bytes 2359300 | tf_op jit(solution)/shard_map/while
  139.0 8.3 %copy-start.26 = (f32[896,3]{0,1:T(4,128)S(1)}, f32[896,3]{0,1:T(4,128)}, u32[]{:S(2)}) copy-start(f32[896,3]{0,1:T(4,128)} %copy-done.25) | copy-start | bytes 32260 | tf_op jit(solution)/shard_map/while
  139.0 8.3 %copy-start.29 = (s32[12,3]{0,1:T(4,128)S(1)}, s32[12,3]{0,1:T(4,128)}, u32[]{:S(2)}) copy-start(s32[12,3]{0,1:T(4,128)} %get-tuple-element.718) | copy-start | bytes 436 | tf_op jit(solution)/shard_map/while
  139.0 8.3 %copy-start.36 = (s32[8]{0:T(128)S(1)}, s32[8]{0:T(128)}, u32[]{:S(2)}) copy-start(s32[8]{0:T(128)} %get-tuple-element.743) | copy-start | bytes 100 | tf_op jit(solution)/shard_map/while
  139.0 8.3 %copy-start.38 = (s32[9]{0:T(128)S(1)}, s32[9]{0:T(128)}, u32[]{:S(2)}) copy-start(s32[9]{0:T(128)} %get-tuple-element.769) | copy-start | bytes 112 | tf_op jit(solution)/shard_map/while
  163.5 9.5 %copy-start.3 = (f32[192,8,128]{2,0,1:T(8,128)S(1)}, f32[192,8,128]{2,0,1:T(8,128)}, u32[]{:S(2)}) copy-start(f32[192,8,128]{2,0,1:T(8,128)} %slice.481) | copy-start | bytes 2359300 | tf_op jit(solution)/shard_map/while
  175.2 8.1 %copy-start.26 = (f32[896,3]{0,1:T(4,128)S(1)}, f32[896,3]{0,1:T(4,128)}, u32[]{:S(2)}) copy-start(f32[896,3]{0,1:T(4,128)} %copy-done.25) | copy-start | bytes 32260 | tf_op jit(solution)/shard_map/while
  175.2 8.1 %copy-start.29 = (s32[12,3]{0,1:T(4,128)S(1)}, s32[12,3]{0,1:T(4,128)}, u32[]{:S(2)}) copy-start(s32[12,3]{0,1:T(4,128)} %get-tuple-element.718) | copy-start | bytes 436 | tf_op jit(solution)/shard_map/while
  175.2 8.1 %copy-start.36 = (s32[8]{0:T(128)S(1)}, s32[8]{0:T(128)}, u32[]{:S(2)}) copy-start(s32[8]{0:T(128)} %get-tuple-element.743) | copy-start | bytes 100 | tf_op jit(solution)/shard_map/while
  199.6 9.5 %copy-start.3 = (f32[192,8,128]{2,0,1:T(8,128)S(1)}, f32[192,8,128]{2,0,1:T(8,128)}, u32[]{:S(2)}) copy-start(f32[192,8,128]{2,0,1:T(8,128)} %slice.481) | copy-start | bytes 2359300 | tf_op jit(solution)/shard_map/while
  211.2 8.3 %copy-start.26 = (f32[896,3]{0,1:T(4,128)S(1)}, f32[896,3]{0,1:T(4,128)}, u32[]{:S(2)}) copy-start(f32[896,3]{0,1:T(4,128)} %copy-done.25) | copy-start | bytes 32260 | tf_op jit(solution)/shard_map/while
  211.2 8.3 %copy-start.29 = (s32[12,3]{0,1:T(4,128)S(1)}, s32[12,3]{0,1:T(4,128)}, u32[]{:S(2)}) copy-start(s32[12,3]{0,1:T(4,128)} %get-tuple-element.718) | copy-start | bytes 436 | tf_op jit(solution)/shard_map/while
  211.2 8.3 %copy-start.36 = (s32[8]{0:T(128)S(1)}, s32[8]{0:T(128)}, u32[]{:S(2)}) copy-start(s32[8]{0:T(128)} %get-tuple-element.743) | copy-start | bytes 100 | tf_op jit(solution)/shard_map/while
  211.2 8.3 %copy-start.38 = (s32[9]{0:T(128)S(1)}, s32[9]{0:T(128)}, u32[]{:S(2)}) copy-start(s32[9]{0:T(128)} %get-tuple-element.769) | copy-start | bytes 112 | tf_op jit(solution)/shard_map/while
  235.8 9.5 %copy-start.3 = (f32[192,8,128]{2,0,1:T(8,128)S(1)}, f32[192,8,128]{2,0,1:T(8,128)}, u32[]{:S(2)}) copy-start(f32[192,8,128]{2,0,1:T(8,128)} %slice.481) | copy-start | bytes 2359300 | tf_op jit(solution)/shard_map/while
  247.4 8.2 %copy-start.26 = (f32[896,3]{0,1:T(4,128)S(1)}, f32[896,3]{0,1:T(4,128)}, u32[]{:S(2)}) copy-start(f32[896,3]{0,1:T(4,128)} %copy-done.25) | copy-start | bytes 32260 | tf_op jit(solution)/shard_map/while
  247.4 8.1 %copy-start.29 = (s32[12,3]{0,1:T(4,128)S(1)}, s32[12,3]{0,1:T(4,128)}, u32[]{:S(2)}) copy-start(s32[12,3]{0,1:T(4,128)} %get-tuple-element.718) | copy-start | bytes 436 | tf_op jit(solution)/shard_map/while
  247.4 8.1 %copy-start.36 = (s32[8]{0:T(128)S(1)}, s32[8]{0:T(128)}, u32[]{:S(2)}) copy-start(s32[8]{0:T(128)} %get-tuple-element.743) | copy-start | bytes 100 | tf_op jit(solution)/shard_map/while
  271.8 9.5 %copy-start.3 = (f32[192,8,128]{2,0,1:T(8,128)S(1)}, f32[192,8,128]{2,0,1:T(8,128)}, u32[]{:S(2)}) copy-start(f32[192,8,128]{2,0,1:T(8,128)} %slice.481) | copy-start | bytes 2359300 | tf_op jit(solution)/shard_map/while
  283.4 8.3 %copy-start.26 = (f32[896,3]{0,1:T(4,128)S(1)}, f32[896,3]{0,1:T(4,128)}, u32[]{:S(2)}) copy-start(f32[896,3]{0,1:T(4,128)} %copy-done.25) | copy-start | bytes 32260 | tf_op jit(solution)/shard_map/while
  283.4 8.3 %copy-start.29 = (s32[12,3]{0,1:T(4,128)S(1)}, s32[12,3]{0,1:T(4,128)}, u32[]{:S(2)}) copy-start(s32[12,3]{0,1:T(4,128)} %get-tuple-element.718) | copy-start | bytes 436 | tf_op jit(solution)/shard_map/while
  283.4 8.3 %copy-start.36 = (s32[8]{0:T(128)S(1)}, s32[8]{0:T(128)}, u32[]{:S(2)}) copy-start(s32[8]{0:T(128)} %get-tuple-element.743) | copy-start | bytes 100 | tf_op jit(solution)/shard_map/while
  283.4 8.3 %copy-start.38 = (s32[9]{0:T(128)S(1)}, s32[9]{0:T(128)}, u32[]{:S(2)}) copy-start(s32[9]{0:T(128)} %get-tuple-element.769) | copy-start | bytes 112 | tf_op jit(solution)/shard_map/while
  308.0 9.5 %copy-start.3 = (f32[192,8,128]{2,0,1:T(8,128)S(1)}, f32[192,8,128]{2,0,1:T(8,128)}, u32[]{:S(2)}) copy-start(f32[192,8,128]{2,0,1:T(8,128)} %slice.481) | copy-start | bytes 2359300 | tf_op jit(solution)/shard_map/while
  319.6 8.1 %copy-start.26 = (f32[896,3]{0,1:T(4,128)S(1)}, f32[896,3]{0,1:T(4,128)}, u32[]{:S(2)}) copy-start(f32[896,3]{0,1:T(4,128)} %copy-done.25) | copy-start | bytes 32260 | tf_op jit(solution)/shard_map/while
  319.6 8.1 %copy-start.29 = (s32[12,3]{0,1:T(4,128)S(1)}, s32[12,3]{0,1:T(4,128)}, u32[]{:S(2)}) copy-start(s32[12,3]{0,1:T(4,128)} %get-tuple-element.718) | copy-start | bytes 436 | tf_op jit(solution)/shard_map/while
  344.0 9.5 %copy-start.3 = (f32[192,8,128]{2,0,1:T(8,128)S(1)}, f32[192,8,128]{2,0,1:T(8,128)}, u32[]{:S(2)}) copy-start(f32[192,8,128]{2,0,1:T(8,128)} %slice.481) | copy-start | bytes 2359300 | tf_op jit(solution)/shard_map/while
  355.6 8.3 %copy-start.26 = (f32[896,3]{0,1:T(4,128)S(1)}, f32[896,3]{0,1:T(4,128)}, u32[]{:S(2)}) copy-start(f32[896,3]{0,1:T(4,128)} %copy-done.25) | copy-start | bytes 32260 | tf_op jit(solution)/shard_map/while
  355.6 8.3 %copy-start.29 = (s32[12,3]{0,1:T(4,128)S(1)}, s32[12,3]{0,1:T(4,128)}, u32[]{:S(2)}) copy-start(s32[12,3]{0,1:T(4,128)} %get-tuple-element.718) | copy-start | bytes 436 | tf_op jit(solution)/shard_map/while
  355.6 8.3 %copy-start.36 = (s32[8]{0:T(128)S(1)}, s32[8]{0:T(128)}, u32[]{:S(2)}) copy-start(s32[8]{0:T(128)} %get-tuple-element.743) | copy-start | bytes 100 | tf_op jit(solution)/shard_map/while
  355.7 8.3 %copy-start.38 = (s32[9]{0:T(128)S(1)}, s32[9]{0:T(128)}, u32[]{:S(2)}) copy-start(s32[9]{0:T(128)} %get-tuple-element.769) | copy-start | bytes 112 | tf_op jit(solution)/shard_map/while
  380.2 9.5 %copy-start.3 = (f32[192,8,128]{2,0,1:T(8,128)S(1)}, f32[192,8,128]{2,0,1:T(8,128)}, u32[]{:S(2)}) copy-start(f32[192,8,128]{2,0,1:T(8,128)} %slice.481) | copy-start | bytes 2359300 | tf_op jit(solution)/shard_map/while
  391.8 8.1 %copy-start.26 = (f32[896,3]{0,1:T(4,128)S(1)}, f32[896,3]{0,1:T(4,128)}, u32[]{:S(2)}) copy-start(f32[896,3]{0,1:T(4,128)} %copy-done.25) | copy-start | bytes 32260 | tf_op jit(solution)/shard_map/while
  391.8 8.1 %copy-start.29 = (s32[12,3]{0,1:T(4,128)S(1)}, s32[12,3]{0,1:T(4,128)}, u32[]{:S(2)}) copy-start(s32[12,3]{0,1:T(4,128)} %get-tuple-element.718) | copy-start | bytes 436 | tf_op jit(solution)/shard_map/while
  416.2 9.5 %copy-start.3 = (f32[192,8,128]{2,0,1:T(8,128)S(1)}, f32[192,8,128]{2,0,1:T(8,128)}, u32[]{:S(2)}) copy-start(f32[192,8,128]{2,0,1:T(8,128)} %slice.481) | copy-start | bytes 2359300 | tf_op jit(solution)/shard_map/while
  427.8 8.3 %copy-start.26 = (f32[896,3]{0,1:T(4,128)S(1)}, f32[896,3]{0,1:T(4,128)}, u32[]{:S(2)}) copy-start(f32[896,3]{0,1:T(4,128)} %copy-done.25) | copy-start | bytes 32260 | tf_op jit(solution)/shard_map/while
  427.8 8.3 %copy-start.29 = (s32[12,3]{0,1:T(4,128)S(1)}, s32[12,3]{0,1:T(4,128)}, u32[]{:S(2)}) copy-start(s32[12,3]{0,1:T(4,128)} %get-tuple-element.718) | copy-start | bytes 436 | tf_op jit(solution)/shard_map/while
  427.8 8.3 %copy-start.36 = (s32[8]{0:T(128)S(1)}, s32[8]{0:T(128)}, u32[]{:S(2)}) copy-start(s32[8]{0:T(128)} %get-tuple-element.743) | copy-start | bytes 100 | tf_op jit(solution)/shard_map/while
  427.9 8.3 %copy-start.38 = (s32[9]{0:T(128)S(1)}, s32[9]{0:T(128)}, u32[]{:S(2)}) copy-start(s32[9]{0:T(128)} %get-tuple-element.769) | copy-start | bytes 112 | tf_op jit(solution)/shard_map/while
  452.4 9.5 %copy-start.3 = (f32[192,8,128]{2,0,1:T(8,128)S(1)}, f32[192,8,128]{2,0,1:T(8,128)}, u32[]{:S(2)}) copy-start(f32[192,8,128]{2,0,1:T(8,128)} %slice.481) | copy-start | bytes 2359300 | tf_op jit(solution)/shard_map/while
  488.4 9.5 %copy-start.3 = (f32[192,8,128]{2,0,1:T(8,128)S(1)}, f32[192,8,128]{2,0,1:T(8,128)}, u32[]{:S(2)}) copy-start(f32[192,8,128]{2,0,1:T(8,128)} %slice.481) | copy-start | bytes 2359300 | tf_op jit(solution)/shard_map/while
  500.0 8.2 %copy-start.26 = (f32[896,3]{0,1:T(4,128)S(1)}, f32[896,3]{0,1:T(4,128)}, u32[]{:S(2)}) copy-start(f32[896,3]{0,1:T(4,128)} %copy-done.25) | copy-start | bytes 32260 | tf_op jit(solution)/shard_map/while
  500.0 8.2 %copy-start.29 = (s32[12,3]{0,1:T(4,128)S(1)}, s32[12,3]{0,1:T(4,128)}, u32[]{:S(2)}) copy-start(s32[12,3]{0,1:T(4,128)} %get-tuple-element.718) | copy-start | bytes 436 | tf_op jit(solution)/shard_map/while
  500.0 8.2 %copy-start.36 = (s32[8]{0:T(128)S(1)}, s32[8]{0:T(128)}, u32[]{:S(2)}) copy-start(s32[8]{0:T(128)} %get-tuple-element.743) | copy-start | bytes 100 | tf_op jit(solution)/shard_map/while
  500.0 8.2 %copy-start.38 = (s32[9]{0:T(128)S(1)}, s32[9]{0:T(128)}, u32[]{:S(2)}) copy-start(s32[9]{0:T(128)} %get-tuple-element.769) | copy-start | bytes 112 | tf_op jit(solution)/shard_map/while
  508.9 5.1 collective-permute-start.4
  511.6 9.1 %collective-permute-start.5 = (f32[64,3]{0,1:T(4,128)S(1)}, f32[64,3]{0,1:T(4,128)S(1)}, u32[]{:S(2)}, u32[]{:S(2)}) collective-permute-start(f32[64,3]{0,1:T(4,128)S(1)} %get-tuple-element.461), channel_id=1, source_target_pairs={{1,0},{2,1},{3,2},{4,3},{5,4},{6,5},{7,6},{8,7},{9,8},{10,9},{11,1... | collective-permute-start | bytes 2312 | tf_op jit(solution)/shard_map/ppermute | solution.py:25
  (302 other events, 1028.8 us)
where the time goes:
time: 529 us; the launch traced here: 522 us
  other arithmetic  198 us (37%)
  matrix products  162 us (31%)
  local copies, waits for them, and re-layouts  102 us (19%)
  starting transfers between devices  27.8 us (5%)
  waiting for transfers between devices  23.7 us (4%)
  loops' own time  7.81 us (1%)
    dot_general x24, matrix products, block_messages(): jnp.einsum('nyij,njyc->ic', edges, dot_terms, preferred_element_type=jnp....  50.9 us
    dot_general x24, matrix products, block_messages(): jnp.einsum('nij,njyc->yic', edges[:, 0], carry_terms, preferred_element_t...  36.5 us
    dot_general x24, matrix products, atom_outputs(): jnp.dot(rounded, mix_weight, preferred_element_type=jnp.float32)  30.8 us
    while x708, local copies, waits for them, and re-layouts  29 us
    reduce_sum x12, other arithmetic, edge_factors(): radial = envelope[None] * jnp.cos(orders[:, None, None] * spread[None])  26.3 us
    select_n x12, other arithmetic, pair_mask(): jnp.where(columns < block_rows, listed[0], jnp.where(columns < 2 * block_...  22.4 us
    mul x12, other arithmetic, edge_factors(): radial = envelope[None] * jnp.cos(orders[:, None, None] * spread[None])  21 us
    dynamic_update_slice x12, other arithmetic, one_block(): energies = lax.dynamic_update_slice_in_dim(energies, energy, start_row, 0)  17.4 us
  transfers between devices with their start and end apart: 7, of which 3 were waited for; matrix products, arithmetic and copies ran while one was open for 4% of the time, Pallas kernels for 0%

commit v1 on v0

v1 whole, which is shorter than its diff:
```python
import functools
import math

import jax
import jax.numpy as jnp
import numpy as np
from jax import lax
from jax.experimental import pallas as pl
from jax.experimental.pallas import tpu as pltpu
from jax.sharding import PartitionSpec as P

BLOCK = 64
CH = 128
ROOT_THREE = math.sqrt(3.0)
DOT_PATH = (0, 5, 5, 5, 6, 6, 6, 6, 6)
CARRY_PATH = (-1, 3, 3, 3, 4, 4, 4, 4, 4)
LIFT_PATH = (-1, 1, 1, 1, 2, 2, 2, 2, 2)
CHUNK = 16
NB = 8
F32 = jnp.float32
BF16 = jnp.bfloat16


def mm(a, b):
    return jnp.dot(a, b, preferred_element_type=F32)


def mm_t(a, b):
    return lax.dot_general(a, b, (((1,), (1,)), ((), ())), preferred_element_type=F32)


def sin_pi(u):
    u2 = u * u
    acc = jnp.full_like(u, -(math.pi**11) / math.factorial(11))
    for power in (9, 7, 5, 3, 1):
        sign = 1.0 if power % 4 == 1 else -1.0
        acc = acc * u2 + sign * math.pi**power / math.factorial(power)
    return acc * u


def cos_pi(u):
    u2 = u * u
    acc = jnp.full_like(u, math.pi**12 / math.factorial(12))
    for power in (10, 8, 6, 4, 2, 0):
        sign = 1.0 if power % 4 == 0 else -1.0
        acc = acc * u2 + sign * math.pi**power / math.factorial(power)
    return acc


def harmonics(dx, dy, dz, x2, y2, z2):
    return (
        None,
        dx,
        dy,
        dz,
        ROOT_THREE * (dx * dy),
        ROOT_THREE * (dy * dz),
        z2 - 0.5 * (x2 + y2),
        ROOT_THREE * (dz * dx),
        (0.5 * ROOT_THREE) * (x2 - y2),
    )


def geometry(e, row0, pos_i, pos_j, keep):
    start = pl.multiple_of(e * BLOCK + row0, CHUNK)
    centre = pos_i[pl.ds(start, CHUNK), :]
    nbr = pos_j[e]
    dx = nbr[0:1, :] - centre[:, 0:1]
    dy = nbr[1:2, :] - centre[:, 1:2]
    dz = nbr[2:3, :] - centre[:, 2:3]
    x2, y2, z2 = dx * dx, dy * dy, dz * dz
    s = x2 + y2 + z2
    t = jnp.maximum(1.0 - s, 0.0)
    mask = keep[e * 3 + row0 // BLOCK]
    t2 = t * t * mask
    if row0 // BLOCK == 1:
        row = lax.broadcasted_iota(jnp.int32, (CHUNK, CH), 0) + row0 % BLOCK
        col = lax.broadcasted_iota(jnp.int32, (CHUNK, CH), 1) % BLOCK
        t2 = jnp.where(row == col, 0.0, t2)
    return dx, dy, dz, x2, y2, z2, s, t, t2


def build_edges(e, pos_i, pos_j, keep, edges):
    odd = lax.broadcasted_iota(jnp.int32, (CHUNK, CH), 1) >= BLOCK
    for row0 in range(0, 3 * BLOCK, CHUNK):
        dx, dy, dz, x2, y2, z2, s, t, t2 = geometry(e, row0, pos_i, pos_j, keep)
        env = t2 * t
        ys = harmonics(dx, dy, dz, x2, y2, z2)
        c1 = -sin_pi(jnp.minimum(s, 1.0) - 0.5)
        c2 = 2.0 * c1 * c1 - 1.0
        two_c2 = 2.0 * c2
        before = env * jnp.where(odd, c1, c2)
        now = env * jnp.where(odd, c1, 1.0)
        for m in range(4):
            cols = slice(m * CH, (m + 1) * CH)
            rows = slice(row0, row0 + CHUNK)
            edges[0, rows, cols] = now.astype(BF16)
            for k in range(1, 9):
                edges[k, rows, cols] = (now * ys[k]).astype(BF16)
            before, now = now, two_c2 * now - before


def build_terms(e, feats, weights, terms, terms0):
    for row0 in range(0, BLOCK, CHUNK):
        start = pl.multiple_of(e * BLOCK + row0, CHUNK)
        h0 = feats[pl.ds(start, CHUNK), 0:CH].astype(F32)
        for n in range(NB):
            rows = slice(n * BLOCK + row0, n * BLOCK + row0 + CHUNK)
            terms0[rows, 0:CH] = (h0 * weights[n, 0:1, :]).astype(BF16)
            for q in range(2):
                terms[rows, (8 + q) * CH : (9 + q) * CH] = (
                    h0 * weights[n, 1 + q : 2 + q, :]
                ).astype(BF16)
        for k in range(1, 9):
            hk = feats[pl.ds(start, CHUNK), k * CH : (k + 1) * CH].astype(F32)
            for n in range(NB):
                rows = slice(n * BLOCK + row0, n * BLOCK + row0 + CHUNK)
                dot_w = weights[n, DOT_PATH[k] : DOT_PATH[k] + 1, :]
                carry_w = weights[n, CARRY_PATH[k] : CARRY_PATH[k] + 1, :]
                terms[rows, (k - 1) * CH : k * CH] = (hk * dot_w).astype(BF16)
                terms0[rows, k * CH : (k + 1) * CH] = (hk * carry_w).astype(BF16)


def pair_terms(terms, k):
    q = LIFT_PATH[k] - 1
    return jnp.concatenate(
        [terms[:, (k - 1) * CH : k * CH], terms[:, (8 + q) * CH : (9 + q) * CH]], axis=1
    )


def block_kernel(
    keep,
    count,
    pos_i,
    pos_j,
    feats,
    gains,
    weights,
    mix,
    self_w,
    readout,
    cols_out,
    nbr_out,
    new_out,
    edges,
    terms,
    terms0,
    msg,
    dmsg,
    rad,
    drad,
    harm,
    gharm,
    accum,
    cols,
):
    ext_blocks = pos_j.shape[0]
    own_blocks = ext_blocks - 2
    width = 3 * BLOCK

    msg[...] = jnp.zeros_like(msg)
    dmsg[...] = jnp.zeros_like(dmsg)
    cols[...] = jnp.zeros_like(cols)

    def forward(e, carry):
        build_edges(e, pos_i, pos_j, keep, edges)
        build_terms(e, feats, weights, terms, terms0)
        rows = pl.ds(pl.multiple_of(e * BLOCK, BLOCK), width)
        total = mm(edges[0], terms0[:, 0:CH])
        for k in range(1, 9, 2):
            carried = mm(edges[0], terms0[:, k * CH : (k + 2) * CH])
            for step in range(2):
                both = mm(edges[k + step], pair_terms(terms, k + step))
                total += both[:, 0:CH]
                msg[k + step, rows, :] += both[:, CH:] + carried[:, step * CH : (step + 1) * CH]
        msg[0, rows, :] += total
        return carry

    lax.fori_loop(0, ext_blocks, forward, 0)

    def atoms(b, carry):
        rows = pl.ds(pl.multiple_of((b + 2) * BLOCK, BLOCK), BLOCK)
        own = pl.ds(pl.multiple_of(b * BLOCK, BLOCK), BLOCK)
        ext = pl.ds(pl.multiple_of((b + 1) * BLOCK, BLOCK), BLOCK)
        live = (lax.broadcasted_iota(jnp.int32, (BLOCK, 1), 0) < count[b]).astype(F32)
        m = [msg[k, rows, :] for k in range(9)]
        first = m[1] * m[1] + m[2] * m[2] + m[3] * m[3]
        second = m[4] * m[4] + m[5] * m[5] + m[6] * m[6] + m[7] * m[7] + m[8] * m[8]
        g0, g1, g2 = (gains[own, l * CH : (l + 1) * CH] for l in range(3))
        basis = m[0] + g0 * (m[0] * m[0]) + g1 * first + g2 * second
        mixed = mm(basis.astype(BF16), mix[...]) + mm(feats[ext, 0:CH], self_w[...])
        new_out[own, :] = (mixed * live).astype(BF16)
        gate = 1.0 / (1.0 + jnp.exp(-mixed))
        value = mixed * gate
        energy = live * jnp.sum(readout[...] * value, axis=1, keepdims=True)
        slope = live * readout[...] * (gate + value * (1.0 - gate))
        dbasis = mm_t(slope.astype(BF16), mix[...]).astype(BF16).astype(F32)
        dmsg[rows, 0:CH] = (dbasis * (1.0 + 2.0 * g0 * m[0])).astype(BF16)
        for k in range(1, 9):
            gain = g1 if k < 4 else g2
            dmsg[rows, k * CH : (k + 1) * CH] = (2.0 * dbasis * gain * m[k]).astype(BF16)
        lane = lax.broadcasted_iota(jnp.int32, (BLOCK, CH), 1)
        cols[rows, :] = jnp.where(lane == 3, energy, 0.0)
        return carry

    lax.fori_loop(0, own_blocks, atoms, 0)

    lane_row = lax.broadcasted_iota(jnp.int32, (1, CH), 1)
    parity = (lane_row >= BLOCK).astype(F32)

    def backward(e, carry):
        build_terms(e, feats, weights, terms, terms0)
        odd = lax.broadcasted_iota(jnp.int32, (CHUNK, CH), 1) >= BLOCK
        for row0 in range(0, width, CHUNK):
            dx, dy, dz, x2, y2, z2, s, t, t2 = geometry(e, row0, pos_i, pos_j, keep)
            env = t2 * t
            denv = -3.0 * t2
            ys = harmonics(dx, dy, dz, x2, y2, z2)
            u = jnp.minimum(s, 1.0) - 0.5
            c1 = -sin_pi(u)
            s1 = cos_pi(u)
            c2 = 2.0 * c1 * c1 - 1.0
            s2 = 2.0 * c1 * s1
            two_c2 = 2.0 * c2
            c_before, c_now = jnp.where(odd, c1, c2), jnp.where(odd, c1, 1.0)
            s_before, s_now = jnp.where(odd, -s1, -s2), jnp.where(odd, s1, 0.0)
            rows = slice(row0, row0 + CHUNK)
            for m in range(4):
                sl = slice(m * CH, (m + 1) * CH)
                order = math.pi * (2.0 * m + parity)
                rad[rows, sl] = env * c_now
                drad[rows, sl] = denv * c_now - env * (order * s_now)
                c_before, c_now = c_now, two_c2 * c_now - c_before
                s_before, s_now = s_now, two_c2 * s_now - s_before
            for k in range(1, 9):
                harm[k, rows, :] = ys[k]
        centre = pl.ds(pl.multiple_of(e * BLOCK, BLOCK), width)
        grad = mm_t(dmsg[centre, :], terms0[...])
        total = None
        for m in range(4):
            sl = slice(m * CH, (m + 1) * CH)
            part = drad[:, sl] * grad[:, sl]
            total = part if total is None else total + part
        accum[...] = total
        for k in range(1, 9):
            lhs = jnp.concatenate(
                [dmsg[centre, 0:CH], dmsg[centre, k * CH : (k + 1) * CH]], axis=1
            )
            grad = mm_t(lhs, pair_terms(terms, k))
            by_r = None
            by_y = None
            for m in range(4):
                sl = slice(m * CH, (m + 1) * CH)
                part_r = drad[:, sl] * grad[:, sl]
                part_y = rad[:, sl] * grad[:, sl]
                by_r = part_r if by_r is None else by_r + part_r
                by_y = part_y if by_y is None else by_y + part_y
            accum[...] += harm[k] * by_r
            gharm[k] = by_y
        tot = [jnp.zeros((CHUNK, CH), F32) for _ in range(3)]
        lane = lax.broadcasted_iota(jnp.int32, (CHUNK, CH), 1)
        for row0 in range(0, width, CHUNK):
            rows = slice(row0, row0 + CHUNK)
            dx, dy, dz = (harm[k, rows, :] for k in (1, 2, 3))
            gy = [None] + [gharm[k, rows, :] for k in range(1, 9)]
            radial = 2.0 * accum[rows, :]
            gx = dx * (radial - gy[6]) + gy[1] + ROOT_THREE * (dy * gy[4] + dz * gy[7] + dx * gy[8])
            gyy = dy * (radial - gy[6]) + gy[2] + ROOT_THREE * (dx * gy[4] + dz * gy[5] - dy * gy[8])
            gz = dz * (radial + 2.0 * gy[6]) + gy[3] + ROOT_THREE * (dy * gy[5] + dx * gy[7])
            parts = (gx, gyy, gz)
            tot = [a + b for a, b in zip(tot, parts)]
            sums = [jnp.sum(p, axis=1, keepdims=True) for p in parts]
            add = jnp.where(lane == 0, sums[0], jnp.where(lane == 1, sums[1], jnp.where(lane == 2, sums[2], 0.0)))
            at = pl.ds(pl.multiple_of(e * BLOCK + row0, CHUNK), CHUNK)
            cols[at, :] += add
        sub = lax.broadcasted_iota(jnp.int32, (8, CH), 0)
        col_sums = [jnp.sum(p, axis=0, keepdims=True) for p in tot]
        nbr_out[e] = jnp.where(
            sub == 0, col_sums[0], jnp.where(sub == 1, col_sums[1], jnp.where(sub == 2, col_sums[2], 0.0))
        )
        return carry

    lax.fori_loop(0, ext_blocks, backward, 0)
    cols_out[...] = jnp.transpose(cols[...])[0:8, :]


def block_stage(keep, count, pos_i, pos_j, feats, gains, weights, mix, self_w, readout):
    ext_blocks = pos_j.shape[0]
    own_rows = (ext_blocks - 2) * BLOCK
    pad_rows = pos_i.shape[0]
    vmem = pl.BlockSpec(memory_space=pltpu.VMEM)
    smem = pl.BlockSpec(memory_space=pltpu.SMEM)
    width = 3 * BLOCK
    return pl.pallas_call(
        block_kernel,
        out_shape=(
            jax.ShapeDtypeStruct((8, pad_rows), F32),
            jax.ShapeDtypeStruct((ext_blocks, 8, CH), F32),
            jax.ShapeDtypeStruct((own_rows, CH), BF16),
        ),
        in_specs=[smem, smem] + [vmem] * 8,
        out_specs=(vmem, vmem, vmem),
        scratch_shapes=[
            pltpu.VMEM((9, width, NB * BLOCK), BF16),
            pltpu.VMEM((NB * BLOCK, 10 * CH), BF16),
            pltpu.VMEM((NB * BLOCK, 9 * CH), BF16),
            pltpu.VMEM((9, pad_rows, CH), F32),
            pltpu.VMEM((pad_rows, 9 * CH), BF16),
            pltpu.VMEM((width, NB * BLOCK), F32),
            pltpu.VMEM((width, NB * BLOCK), F32),
            pltpu.VMEM((9, width, CH), F32),
            pltpu.VMEM((9, width, CH), F32),
            pltpu.VMEM((width, CH), F32),
            pltpu.VMEM((pad_rows, CH), F32),
        ],
        compiler_params=pltpu.CompilerParams(vmem_limit_bytes=50 * 1024 * 1024),
        name="block_stage",
    )(keep, count, pos_i, pos_j, feats, gains, weights, mix, self_w, readout)


def gather_kernel(arrival, count, rows_in, out):
    atom_rows = arrival.shape[0]
    source = rows_in.shape[0]
    index = arrival[...]
    slot = (index // 6) * 8 + index % 6
    lane = lax.broadcasted_iota(jnp.int32, (atom_rows, source), 1)
    pick = jnp.where(slot == lane, count[...], 0.0).astype(BF16)
    for k in range(9):
        out[:, k * CH : (k + 1) * CH] = mm(pick, rows_in[:, k * CH : (k + 1) * CH]).astype(BF16)


def gather_stage(arrival, live, rows_in):
    atom_rows = arrival.shape[0]
    vmem = pl.BlockSpec(memory_space=pltpu.VMEM)
    return pl.pallas_call(
        gather_kernel,
        out_shape=jax.ShapeDtypeStruct((atom_rows, rows_in.shape[1]), BF16),
        in_specs=[vmem] * 3,
        out_specs=vmem,
        compiler_params=pltpu.CompilerParams(vmem_limit_bytes=32 * 1024 * 1024),
        name="gather_stage",
    )(arrival, live, rows_in)


def ring_pairs(axes):
    count = math.prod(lax.axis_size(axis) for axis in axes)
    forward = [(i, i + 1) for i in range(count - 1)]
    backward = [(target, source) for source, target in forward]
    return forward, backward


def per_device(
    features_domain,
    arrival,
    positions,
    species,
    block_count,
    pair_block,
    radial_weights,
    species_weights,
    mix_weight,
    self_weight,
    readout,
):
    axes = ("dom", "blk")
    devices = lax.axis_size(axes)
    atom_rows, feature_cols = features_domain.shape
    piece = atom_rows // devices
    blocks = atom_rows // BLOCK
    forward, backward = ring_pairs(axes)

    parcels = jnp.pad(
        features_domain.reshape(devices, piece, feature_cols), ((0, 0), (0, 8 - piece), (0, 0))
    )
    received = lax.all_to_all(parcels, axes, split_axis=0, concat_axis=0, tiled=True)
    received = received.reshape(devices * 8, feature_cols)

    coords = positions.T
    low = lax.ppermute(coords[:, atom_rows - BLOCK :], axes, forward)
    high = lax.ppermute(coords[:, :BLOCK], axes, backward)
    coords_ext = jnp.concatenate([low, coords, high], axis=1)
    pos_i = jnp.pad(coords_ext, ((0, 5), (BLOCK, BLOCK))).T
    by_block = coords_ext.reshape(3, blocks + 2, BLOCK).transpose(1, 0, 2)
    pos_j = jnp.pad(jnp.concatenate([by_block, by_block], axis=2), ((0, 0), (0, 5), (0, 0)))
    listed = jnp.pad((pair_block >= 0).astype(F32), ((2, 2), (0, 0)))
    keep = jnp.stack(
        [listed[0 : blocks + 2, 2], listed[1 : blocks + 3, 1], listed[2 : blocks + 4, 0]], axis=1
    ).reshape(-1)
    live = (jnp.arange(BLOCK, dtype=jnp.int32)[None, :] < block_count[:, None]).astype(F32)
    total = species_weights.shape[0]
    one_hot = (species[:, None] == jnp.arange(total, dtype=jnp.int32)[None, :]).astype(F32)
    gains = jnp.dot(one_hot, species_weights.reshape(total, -1), precision=lax.Precision.HIGHEST)

    relaid = gather_stage(arrival[:, None], live.reshape(atom_rows, 1), received)
    below = lax.ppermute(relaid[atom_rows - BLOCK :], axes, forward)
    above = lax.ppermute(relaid[:BLOCK], axes, backward)
    feats = jnp.concatenate([below, relaid, above], axis=0)

    cols, nbr, new_rows = block_stage(
        keep,
        block_count,
        pos_i,
        pos_j,
        feats,
        gains,
        radial_weights,
        mix_weight,
        self_weight,
        readout[None, :],
    )
    energies = cols[3, 2 * BLOCK : 2 * BLOCK + atom_rows]
    on_nbr = nbr[:, 0:3, :BLOCK] + nbr[:, 0:3, BLOCK:]
    from_low = lax.ppermute(on_nbr[blocks + 1], axes, forward)
    from_high = lax.ppermute(on_nbr[0], axes, backward)
    own = on_nbr[1 : blocks + 1]
    own = own.at[0].add(from_low).at[blocks - 1].add(from_high)
    own = own.transpose(1, 0, 2).reshape(3, atom_rows)
    forces = (cols[0:3, 2 * BLOCK : 2 * BLOCK + atom_rows] - own).T
    return (energies, forces, new_rows)


def solution(mesh):
    placed = (
        P(("dom", "blk"), None),
        P(("dom", "blk")),
        P(("dom", "blk"), None),
        P(("dom", "blk")),
        P(("dom", "blk")),
        P(("dom", "blk"), None),
        P(),
        P(),
        P(),
        P(),
        P(),
    )
    return jax.shard_map(
        per_device,
        mesh=mesh,
        in_specs=placed,
        out_specs=(P(("dom", "blk")), P(("dom", "blk"), None), P(("dom", "blk"), None)),
        check_vma=False,
    )
```

time: 529 us -> 136 us (0.26); the launches traced: 522 us -> 135 us
  other arithmetic: 198 us -> 3.98 us
  matrix products: 162 us -> 0.68 us
  local copies, waits for them, and re-layouts: 102 us -> 19.2 us
  Pallas kernels: 0 us -> 55.8 us
  loops' own time: 7.81 us -> 0 us
    dot_general x133 -> x1, matrix products: 162 us -> 0.68 us  [per_device(): jnp.dot(one_hot, species_weights.reshape(total, -1), precision=lax.Precis...]
    pallas_call x0 -> x2, Pallas kernels: none -> 55.8 us  [the longest x1 51.7 us: block_stage(): pl.pallas_call(block_kernel, out_shape=(jax.ShapeDtypeStruct((8, pad_rows...]
    reduce_sum x72 -> x0, other arithmetic: 47.2 us -> none  [the longest x12 26.3 us: edge_factors(): radial = envelope[None] * jnp.cos(orders[:, None, None] * spread[None])]
    mul x60 -> x0, other arithmetic: 32.5 us -> none  [the longest x12 21 us: edge_factors(): radial = envelope[None] * jnp.cos(orders[:, None, None] * spread[None])]
    while x708 -> x0, local copies, waits for them, and re-layouts: 29 us -> none
    convert_element_type x49 -> x1, other arithmetic: 28.6 us -> 0.07 us  [per_device(): (jnp.arange(BLOCK, dtype=jnp.int32)[None, :] < block_count[:, None]).asty...]
    dynamic_update_slice x24 -> x0, other arithmetic: 25.6 us -> none  [the longest x12 17.4 us: one_block(): energies = lax.dynamic_update_slice_in_dim(energies, energy, start_row, 0)]
    select_n x14 -> x0, other arithmetic: 23.5 us -> none  [the longest x12 22.4 us: pair_mask(): jnp.where(columns < block_rows, listed[0], jnp.where(columns < 2 * block_...]
  transfers between devices with their start and end apart: 7 -> 7, of which waited for: 3 -> 4; matrix products, arithmetic and copies ran while one was open for 4% -> 10% of each run, Pallas kernels for 0% -> 0%
where the time goes in v1:
time: 136 us; the launch traced here: 135 us
  Pallas kernels  55.8 us (41%)
  starting transfers between devices  27.9 us (21%)
  waiting for transfers between devices  26.5 us (19%)
  local copies, waits for them, and re-layouts  19.2 us (14%)
  other arithmetic  3.98 us (3%)
    pallas_call x1, Pallas kernels, block_stage(): pl.pallas_call(block_kernel, out_shape=(jax.ShapeDtypeStruct((8, pad_rows...  51.7 us
    ppermute x1, waiting for transfers between devices, per_device(): low = lax.ppermute(coords[:, atom_rows - BLOCK:], axes, forward)  10.3 us
    all_to_all x1, starting transfers between devices, per_device(): lax.all_to_all(parcels, axes, split_axis=0, concat_axis=0, tiled=True)  10.1 us
    ppermute x1, waiting for transfers between devices, per_device(): above = lax.ppermute(relaid[:BLOCK], axes, backward)  7.63 us
    ppermute x1, starting transfers between devices, per_device(): below = lax.ppermute(relaid[atom_rows - BLOCK:], axes, forward)  7.13 us
    ppermute x1, waiting for transfers between devices, per_device(): from_high = lax.ppermute(on_nbr[0], axes, backward)  6.08 us
    unnamed x28, local copies, waits for them, and re-layouts  4.78 us
    pallas_call x1, Pallas kernels, gather_stage(): pl.pallas_call(gather_kernel, out_shape=jax.ShapeDtypeStruct((atom_rows,...  4.15 us
  transfers between devices with their start and end apart: 7, of which 4 were waited for; matrix products, arithmetic and copies ran while one was open for 10% of the time, Pallas kernels for 0%

profile of v1, /device:TPU:111, one launch (start us, length us, event | category | flops | bytes accessed | tf_op | source)
XLA Modules:
  0.0 135.1 jit_solution(2989443637330642320)
XLA Ops:
  0.6 2.5 %reshape.118 = bf16[128,6,1152]{2,1,0:T(8,128)(2,1)S(1)} reshape(bf16[768,1152]{1,0:T(8,128)(2,1)} %param.15) | data formatting | bytes 3538944 | tf_op jit(solution)/shard_map/reshape | solution.py:373
  3.2 1.9 %pad.27 = bf16[128,8,1152]{2,1,0:T(8,128)(2,1)} pad(bf16[128,6,1152]{2,1,0:T(8,128)(2,1)S(1)} %reshape.118, bf16[]{:T(256)} %constant.61.clone.1), padding=0_0x0_2x0_0 | pad | bytes 4128770 | tf_op jit(solution)/shard_map/jit(_pad)/pad | solution.py:372
  5.1 0.0 copy-start.8
  5.1 0.0 copy-start.11
  5.1 0.0 copy-start.6
  5.1 0.0 copy-start.10
  5.1 10.1 %all-to-all-start = ((bf16[128,8,1152]{2,1,0:T(8,128)(2,1)}), bf16[128,8,1152]{2,1,0:T(8,128)(2,1)S(1)}, u32[]{:S(2)}, u32[]{:S(2)}) async-start(bf16[128,8,1152]{2,1,0:T(8,128)(2,1)} %pad.27), calls=%async_computation | async-start | bytes 4718592 | tf_op jit(solution)/shard_map/all_to_all | solution.py:375
  15.2 1.4 %fusion.6 = (f32[3,64]{1,0:T(4,128)}, f32[3,64]{1,0:T(4,128)}) fusion(f32[3,768]{1,0:T(4,128)} %bitcast.29), kind=kLoop, calls=%fused_computation.24 | loop fusion | bytes 3072 | tf_op jit(solution)/shard_map/slice | solution.py:379
  16.6 2.6 %collective-permute-start = (f32[3,64]{1,0:T(4,128)}, f32[3,64]{1,0:T(4,128)}, u32[]{:S(2)}, u32[]{:S(2)}) collective-permute-start(f32[3,64]{1,0:T(4,128)} %get-tuple-element.37), channel_id=1, source_target_pairs={{0,1},{1,2},{2,3},{3,4},{4,5},{5,6},{6,7},{7,8},{8,9},{9,10},{10,1... | collective-permute-start | bytes 2312 | tf_op jit(solution)/shard_map/ppermute | solution.py:379
  19.1 1.9 %collective-permute-start.1 = (f32[3,64]{1,0:T(4,128)}, f32[3,64]{1,0:T(4,128)}, u32[]{:S(2)}, u32[]{:S(2)}) collective-permute-start(f32[3,64]{1,0:T(4,128)} %get-tuple-element.38), channel_id=1, source_target_pairs={{1,0},{2,1},{3,2},{4,3},{5,4},{6,5},{7,6},{8,7},{9,8},{10,9},{11,1... | collective-permute-start | bytes 2312 | tf_op jit(solution)/shard_map/ppermute | solution.py:380
  21.0 0.0 copy-done.8
  21.1 0.1 copy.31
  21.2 0.0 copy-done.11
  21.2 0.1 pad_convert_fusion
  21.3 0.1 fusion.7
  21.4 0.0 copy-done.6
  21.4 0.1 fusion.2
  21.5 0.0 copy-done.10
  21.5 0.7 fusion.gains
  22.2 0.7 copy.26
  22.9 0.8 reshape.116.keep
  23.7 1.1 reshape.125.count
  24.7 1.6 %broadcast_in_dim.12.arrival = s32[768,1]{1,0:T(8,128)} reshape(s32[768]{0:T(1024)} %param.16) | data formatting | bytes 6144 | tf_op jit(solution)/shard_map/broadcast_in_dim | solution.py:394
  26.3 1.4 %copy.32.weights = f32[8,7,128]{2,1,0:T(8,128)} copy(f32[8,7,128]{2,0,1:T(8,128)} %param.21) | data formatting | bytes 57344 | tf_op args[6]
  27.7 10.3 %collective-permute-done = f32[3,64]{1,0:T(4,128)} collective-permute-done((f32[3,64]{1,0:T(4,128)}, f32[3,64]{1,0:T(4,128)}, u32[]{:S(2)}, u32[]{:S(2)}) %collective-permute-start) | collective-permute-done | bytes 800 | tf_op jit(solution)/shard_map/ppermute | solution.py:379
  38.1 2.4 %collective-permute-done.1 = f32[3,64]{1,0:T(4,128)} collective-permute-done((f32[3,64]{1,0:T(4,128)}, f32[3,64]{1,0:T(4,128)}, u32[]{:S(2)}, u32[]{:S(2)}) %collective-permute-start.1) | collective-permute-done | bytes 800 | tf_op jit(solution)/shard_map/ppermute | solution.py:380
  40.5 1.4 %pad_maximum_fusion.1 = f32[3,896]{1,0:T(4,128)} fusion(f32[3,64]{1,0:T(4,128)} %collective-permute-done.1, f32[3,768]{1,0:T(4,128)} %bitcast.30, f32[3,64]{1,0:T(4,128)} %collective-permute-done), kind=kLoop, calls=%fused_computation.9 | loop fusion | flops 5376 | bytes 21504 | tf_op jit(solution)/shard_map/concatenate | solution.py:381
  41.9 1.4 %reshape.117 = f32[3,14,64]{2,1,0:T(8,128)} reshape(f32[3,896]{1,0:T(4,128)} %pad_maximum_fusion.1) | data formatting | bytes 21504 | tf_op jit(solution)/shard_map/reshape | solution.py:383
  43.3 1.3 copy.36
  44.6 0.0 all-to-all-done
  44.6 0.0 copy-start.1
  44.6 1.0 copy-done.1
  45.6 0.0 copy-start.2
  45.6 1.0 copy-done.2
  46.6 0.0 copy-start.9
  46.6 4.1 %gather_stage.1 = bf16[768,1152]{1,0:T(8,128)(2,1)S(1)} custom-call(s32[768,1]{1,0:T(8,128)S(1)} %copy-done.2, f32[768,1]{1,0:T(8,128)S(1)} %copy-done.1, bf16[1024,1152]{1,0:T(8,128)(2,1)S(1)} %bitcast.23), custom_call_target="tpu_custom_call" | custom-call | tf_op jit(solution)/shard_map/gather_stage/pallas_call | solution.py:335
  50.8 0.0 copy-start
  50.8 1.2 copy-done
  52.0 7.1 %collective-permute-start.2 = (bf16[64,1152]{1,0:T(8,128)(2,1)S(1)}, bf16[64,1152]{1,0:T(8,128)(2,1)S(1)}, u32[]{:S(2)}, u32[]{:S(2)}) collective-permute-start(bf16[64,1152]{1,0:T(8,128)(2,1)S(1)} %get-tuple-element.33), channel_id=1, source_target_pairs={{0,1},{1,2},{2,3},{3,4},{4,5},{5,6},{6,7},{7,8},{8,9},{9,10},{10,1... | collective-permute-start | bytes 442376 | tf_op jit(solution)/shard_map/ppermute | solution.py:395
  59.2 1.9 %collective-permute-start.3 = (bf16[64,1152]{1,0:T(8,128)(2,1)S(1)}, bf16[64,1152]{1,0:T(8,128)(2,1)S(1)}, u32[]{:S(2)}, u32[]{:S(2)}) collective-permute-start(bf16[64,1152]{1,0:T(8,128)(2,1)S(1)} %get-tuple-element.34), channel_id=1, source_target_pairs={{1,0},{2,1},{3,2},{4,3},{5,4},{6,5},{7,6},{8,7},{9,8},{10,9},{11,1... | collective-permute-start | bytes 442376 | tf_op jit(solution)/shard_map/ppermute | solution.py:396
  61.1 0.0 copy-done.9
  61.1 0.1 select_maximum_fusion.pos_j
  61.2 0.9 copy.27
  62.2 0.0 copy-start.3
  62.2 0.0 copy-start.4
  62.2 0.0 copy-start.5
  62.2 0.0 copy-start.7
  62.2 0.0 collective-permute-done.2
  62.2 7.6 %collective-permute-done.3 = bf16[64,1152]{1,0:T(8,128)(2,1)S(1)} collective-permute-done((bf16[64,1152]{1,0:T(8,128)(2,1)S(1)}, bf16[64,1152]{1,0:T(8,128)(2,1)S(1)}, u32[]{:S(2)}, u32[]{:S(2)}) %collective-permute-start.3) | collective-permute-done | bytes 147488 | tf_op jit(solution)/shard_map/ppermute | solution.py:396
  69.9 1.6 %pad_maximum_fusion.feats = bf16[896,1152]{1,0:T(8,128)(2,1)S(1)} fusion(bf16[64,1152]{1,0:T(8,128)(2,1)S(1)} %collective-permute-done.3, bf16[768,1152]{1,0:T(8,128)(2,1)} %copy-done, bf16[64,1152]{1,0:T(8,128)(2,1)S(1)} %collective-permute-done.2), kind=kLoop, calls=%fused_computation | loop fusion | flops 6193152 | bytes 4128768 | tf_op jit(solution)/shard_map/concatenate | solution.py:397
  71.5 0.0 copy-done.3
  71.5 0.0 copy-done.4
  71.5 0.0 copy-done.5
  71.5 0.0 copy-done.7
  71.5 51.7 %block_stage.1 = (f32[8,1024]{1,0:T(8,128)S(1)}, f32[14,8,128]{2,1,0:T(8,128)S(1)}, bf16[768,128]{1,0:T(8,128)(2,1)}) custom-call(f32[42]{0:T(128)S(1)} %reshape.116.keep, s32[12]{0:T(128)S(1)} %copy-done.6, f32[1024,8]{1,0:T(8,128)S(1)} %pad_bitcast_fusion.pos_i, f32[14,8,128]{2,1,0:T(8,128)S(1)} %select_maximum_fusion.pos_j, ...), custom_call_target="tpu_custom_call" | custom-call | tf_op jit(solution)/shard_map/block_stage/pallas_call | solution.py:294
  123.2 0.1 slice_add_fusion
  123.3 1.9 %collective-permute-start.4 = (f32[3,64]{1,0:T(4,128)S(1)}, f32[3,64]{1,0:T(4,128)S(1)}, u32[]{:S(2)}, u32[]{:S(2)}) collective-permute-start(f32[3,64]{1,0:T(4,128)S(1)} %get-tuple-element.36), channel_id=1, source_target_pairs={{0,1},{1,2},{2,3},{3,4},{4,5},{5,6},{6,7},{7,8},{8,9},{9,10},{10,1... | collective-permute-start | bytes 2312 | tf_op jit(solution)/shard_map/ppermute | solution.py:413
  125.2 2.4 %collective-permute-start.5 = (f32[3,64]{1,0:T(4,128)S(1)}, f32[3,64]{1,0:T(4,128)S(1)}, u32[]{:S(2)}, u32[]{:S(2)}) collective-permute-start(f32[3,64]{1,0:T(4,128)S(1)} %get-tuple-element.35), channel_id=1, source_target_pairs={{1,0},{2,1},{3,2},{4,3},{5,4},{6,5},{7,6},{8,7},{9,8},{10,9},{11,1... | collective-permute-start | bytes 2312 | tf_op jit(solution)/shard_map/ppermute | solution.py:414
  127.7 0.6 slice_reduce_fusion
  128.3 0.0 collective-permute-done.4
  128.3 6.1 %collective-permute-done.5 = f32[3,64]{1,0:T(4,128)S(1)} collective-permute-done((f32[3,64]{1,0:T(4,128)S(1)}, f32[3,64]{1,0:T(4,128)S(1)}, u32[]{:S(2)}, u32[]{:S(2)}) %collective-permute-start.5) | collective-permute-done | bytes 800 | tf_op jit(solution)/shard_map/ppermute | solution.py:414
  134.4 0.1 reshape.123
  134.5 0.6 subtract_bitcast_fusion
  (11 shorter events, 0.2 us)
Async XLA Ops:
  5.1 16.0 %copy-start.8 = (f32[89,3,128]{2,0,1:T(8,128)S(1)}, f32[89,3,128]{2,0,1:T(8,128)}, u32[]{:S(2)}) copy-start(f32[89,3,128]{2,0,1:T(8,128)} %param.22) | copy-start | bytes 410116
  5.1 16.1 %copy-start.11 = (s32[12,3]{0,1:T(4,128)S(1)}, s32[12,3]{0,1:T(4,128)}, u32[]{:S(2)}) copy-start(s32[12,3]{0,1:T(4,128)} %param.20) | copy-start | bytes 436
  5.1 16.3 %copy-start.6 = (s32[12]{0:T(128)S(1)}, s32[12]{0:T(128)}, u32[]{:S(2)}) copy-start(s32[12]{0:T(128)} %count.1) | copy-start | bytes 148
  5.1 16.4 %copy-start.10 = (s32[768]{0:T(1024)S(1)}, s32[768]{0:T(1024)}, u32[]{:S(2)}) copy-start(s32[768]{0:T(1024)} %param.18) | copy-start | bytes 9220
  5.1 39.5 %all-to-all-start = ((bf16[128,8,1152]{2,1,0:T(8,128)(2,1)}), bf16[128,8,1152]{2,1,0:T(8,128)(2,1)S(1)}, u32[]{:S(2)}, u32[]{:S(2)}) async-start(bf16[128,8,1152]{2,1,0:T(8,128)(2,1)} %pad.27), calls=%async_computation | async-start | bytes 4718592 | tf_op jit(solution)/shard_map/all_to_all | solution.py:375
  16.6 21.5 %collective-permute-start = (f32[3,64]{1,0:T(4,128)}, f32[3,64]{1,0:T(4,128)}, u32[]{:S(2)}, u32[]{:S(2)}) collective-permute-start(f32[3,64]{1,0:T(4,128)} %get-tuple-element.37), channel_id=1, source_target_pairs={{0,1},{1,2},{2,3},{3,4},{4,5},{5,6},{6,7},{7,8},{8,9},{9,10},{10,1... | collective-permute-start | bytes 2312 | tf_op jit(solution)/shard_map/ppermute | solution.py:379
  19.1 21.4 %collective-permute-start.1 = (f32[3,64]{1,0:T(4,128)}, f32[3,64]{1,0:T(4,128)}, u32[]{:S(2)}, u32[]{:S(2)}) collective-permute-start(f32[3,64]{1,0:T(4,128)} %get-tuple-element.38), channel_id=1, source_target_pairs={{1,0},{2,1},{3,2},{4,3},{5,4},{6,5},{7,6},{8,7},{9,8},{10,9},{11,1... | collective-permute-start | bytes 2312 | tf_op jit(solution)/shard_map/ppermute | solution.py:380
  44.6 1.0 copy-start.1
  45.6 1.0 copy-start.2
  46.6 14.5 %copy-start.9 = (f32[3,14,64]{2,0,1:T(4,128)S(1)}, f32[3,14,64]{2,0,1:T(4,128)}, u32[]{:S(2)}) copy-start(f32[3,14,64]{2,0,1:T(4,128)} %copy.36) | copy-start | bytes 32260
  50.8 1.2 copy-start
  52.0 10.2 %collective-permute-start.2 = (bf16[64,1152]{1,0:T(8,128)(2,1)S(1)}, bf16[64,1152]{1,0:T(8,128)(2,1)S(1)}, u32[]{:S(2)}, u32[]{:S(2)}) collective-permute-start(bf16[64,1152]{1,0:T(8,128)(2,1)S(1)} %get-tuple-element.33), channel_id=1, source_target_pairs={{0,1},{1,2},{2,3},{3,4},{4,5},{5,6},{6,7},{7,8},{8,9},{9,10},{10,1... | collective-permute-start | bytes 442376 | tf_op jit(solution)/shard_map/ppermute | solution.py:395
  59.2 10.7 %collective-permute-start.3 = (bf16[64,1152]{1,0:T(8,128)(2,1)S(1)}, bf16[64,1152]{1,0:T(8,128)(2,1)S(1)}, u32[]{:S(2)}, u32[]{:S(2)}) collective-permute-start(bf16[64,1152]{1,0:T(8,128)(2,1)S(1)} %get-tuple-element.34), channel_id=1, source_target_pairs={{1,0},{2,1},{3,2},{4,3},{5,4},{6,5},{7,6},{8,7},{9,8},{10,9},{11,1... | collective-permute-start | bytes 442376 | tf_op jit(solution)/shard_map/ppermute | solution.py:396
  62.2 9.3 %copy-start.3 = (f32[8,7,128]{2,1,0:T(8,128)S(1)}, f32[8,7,128]{2,1,0:T(8,128)}, u32[]{:S(2)}) copy-start(f32[8,7,128]{2,1,0:T(8,128)} %copy.32.weights) | copy-start | bytes 86020
  62.2 9.3 %copy-start.4 = (bf16[128,128]{1,0:T(8,128)(2,1)S(1)}, bf16[128,128]{1,0:T(8,128)(2,1)}, u32[]{:S(2)}) copy-start(bf16[128,128]{1,0:T(8,128)(2,1)} %mix.1) | copy-start | bytes 98308
  62.2 9.3 %copy-start.5 = (bf16[128,128]{1,0:T(8,128)(2,1)S(1)}, bf16[128,128]{1,0:T(8,128)(2,1)}, u32[]{:S(2)}) copy-start(bf16[128,128]{1,0:T(8,128)(2,1)} %self_w.1) | copy-start | bytes 98308
  62.2 9.3 %copy-start.7 = (f32[128]{0:T(128)S(1)}, f32[128]{0:T(128)}, u32[]{:S(2)}) copy-start(f32[128]{0:T(128)} %param.25) | copy-start | bytes 1540
  123.3 5.0 %collective-permute-start.4 = (f32[3,64]{1,0:T(4,128)S(1)}, f32[3,64]{1,0:T(4,128)S(1)}, u32[]{:S(2)}, u32[]{:S(2)}) collective-permute-start(f32[3,64]{1,0:T(4,128)S(1)} %get-tuple-element.36), channel_id=1, source_target_pairs={{0,1},{1,2},{2,3},{3,4},{4,5},{5,6},{6,7},{7,8},{8,9},{9,10},{10,1... | collective-permute-start | bytes 2312 | tf_op jit(solution)/shard_map/ppermute | solution.py:413
  125.2 9.1 %collective-permute-start.5 = (f32[3,64]{1,0:T(4,128)S(1)}, f32[3,64]{1,0:T(4,128)S(1)}, u32[]{:S(2)}, u32[]{:S(2)}) collective-permute-start(f32[3,64]{1,0:T(4,128)S(1)} %get-tuple-element.35), channel_id=1, source_target_pairs={{1,0},{2,1},{3,2},{4,3},{5,4},{6,5},{7,6},{8,7},{9,8},{10,9},{11,1... | collective-permute-start | bytes 2312 | tf_op jit(solution)/shard_map/ppermute | solution.py:414

commit v2 on v1

v2 whole, which is shorter than its diff:
```python
import functools
import math

import jax
import jax.numpy as jnp
import numpy as np
from jax import lax
from jax.experimental import pallas as pl
from jax.experimental.pallas import tpu as pltpu
from jax.sharding import PartitionSpec as P

BLOCK = 64
CH = 128
ROOT_THREE = math.sqrt(3.0)
DOT_PATH = (0, 5, 5, 5, 6, 6, 6, 6, 6)
CARRY_PATH = (-1, 3, 3, 3, 4, 4, 4, 4, 4)
LIFT_PATH = (-1, 1, 1, 1, 2, 2, 2, 2, 2)
CHUNK = 16
NB = 8
F32 = jnp.float32
BF16 = jnp.bfloat16


def mm(a, b):
    return jnp.dot(a, b, preferred_element_type=F32)


def mm_t(a, b):
    return lax.dot_general(a, b, (((1,), (1,)), ((), ())), preferred_element_type=F32)


def sin_pi(u):
    u2 = u * u
    acc = jnp.full_like(u, -(math.pi**11) / math.factorial(11))
    for power in (9, 7, 5, 3, 1):
        sign = 1.0 if power % 4 == 1 else -1.0
        acc = acc * u2 + sign * math.pi**power / math.factorial(power)
    return acc * u


def cos_pi(u):
    u2 = u * u
    acc = jnp.full_like(u, math.pi**12 / math.factorial(12))
    for power in (10, 8, 6, 4, 2, 0):
        sign = 1.0 if power % 4 == 0 else -1.0
        acc = acc * u2 + sign * math.pi**power / math.factorial(power)
    return acc


def harmonics(dx, dy, dz, x2, y2, z2):
    return (
        None,
        dx,
        dy,
        dz,
        ROOT_THREE * (dx * dy),
        ROOT_THREE * (dy * dz),
        z2 - 0.5 * (x2 + y2),
        ROOT_THREE * (dz * dx),
        (0.5 * ROOT_THREE) * (x2 - y2),
    )


def geometry(e, row0, pos_i, pos_j, keep):
    start = pl.multiple_of(e * BLOCK + row0, CHUNK)
    centre = pos_i[pl.ds(start, CHUNK), :]
    nbr = pos_j[e]
    dx = nbr[0:1, :] - centre[:, 0:1]
    dy = nbr[1:2, :] - centre[:, 1:2]
    dz = nbr[2:3, :] - centre[:, 2:3]
    x2, y2, z2 = dx * dx, dy * dy, dz * dz
    return dx, dy, dz, x2, y2, z2


def edge_tasks(e, low, width, pos_i, pos_j, keep, put_edge, put_slope):
    def task(row0):
        odd = lax.broadcasted_iota(jnp.int32, (CHUNK, CH), 1) >= BLOCK
        parity = odd.astype(F32)
        dx, dy, dz, x2, y2, z2 = geometry(e, row0, pos_i, pos_j, keep)
        s = x2 + y2 + z2
        t = jnp.maximum(1.0 - s, 0.0)
        t2 = t * t * keep[e * 3 + row0 // BLOCK]
        if row0 // BLOCK == 1:
            row = lax.broadcasted_iota(jnp.int32, (CHUNK, CH), 0) + row0 % BLOCK
            col = lax.broadcasted_iota(jnp.int32, (CHUNK, CH), 1) % BLOCK
            t2 = jnp.where(row == col, 0.0, t2)
        env = t2 * t
        denv = -3.0 * t2
        ys = harmonics(dx, dy, dz, x2, y2, z2)
        u = jnp.minimum(s, 1.0) - 0.5
        c1 = -sin_pi(u)
        s1 = cos_pi(u)
        c2 = 2.0 * c1 * c1 - 1.0
        s2 = 2.0 * c1 * s1
        two_c2 = 2.0 * c2
        c_before, c_now = jnp.where(odd, c1, c2), jnp.where(odd, c1, 1.0)
        s_before, s_now = jnp.where(odd, -s1, -s2), jnp.where(odd, s1, 0.0)
        rows = slice(row0 - low, row0 - low + CHUNK)
        ys = [None] + [y.astype(BF16) for y in ys[1:]]
        for m in range(4):
            cols = slice(m * CH, (m + 1) * CH)
            radial = (env * c_now).astype(BF16)
            order = math.pi * (2.0 * m + parity)
            put_slope(rows, cols, (denv * c_now - env * (order * s_now)).astype(BF16))
            put_edge(0, rows, cols, radial)
            for k in range(1, 9):
                put_edge(k, rows, cols, radial * ys[k])
            c_before, c_now = c_now, two_c2 * c_now - c_before
            s_before, s_now = s_now, two_c2 * s_now - s_before

    return [functools.partial(task, row0) for row0 in range(low, low + width, CHUNK)]


def mingle(main, *others):
    main = list(main)
    queue = [unit for other in others for unit in other]
    done = 0
    for position, step in enumerate(main):
        step()
        upto = len(queue) * (position + 1) // len(main)
        while done < upto:
            queue[done]()
            done += 1


def term_tasks(e, feats, weights, terms, terms0):
    def task(row0, k):
        start = pl.multiple_of(e * BLOCK + row0, CHUNK)
        hk = feats[pl.ds(start, CHUNK), k * CH : (k + 1) * CH]
        for n in range(NB):
            rows = slice(n * BLOCK + row0, n * BLOCK + row0 + CHUNK)
            if k == 0:
                terms0[rows, 0:CH] = hk * weights[n, 0:1, :]
                for q in range(2):
                    terms[rows, (8 + q) * CH : (9 + q) * CH] = hk * weights[n, 1 + q : 2 + q, :]
            else:
                dot_w = weights[n, DOT_PATH[k] : DOT_PATH[k] + 1, :]
                carry_w = weights[n, CARRY_PATH[k] : CARRY_PATH[k] + 1, :]
                terms[rows, (k - 1) * CH : k * CH] = hk * dot_w
                terms0[rows, k * CH : (k + 1) * CH] = hk * carry_w

    return [functools.partial(task, row0, k) for k in range(9) for row0 in range(0, BLOCK, CHUNK)]


def pair_terms(terms, k):
    q = LIFT_PATH[k] - 1
    return jnp.concatenate(
        [terms[:, (k - 1) * CH : k * CH], terms[:, (8 + q) * CH : (9 + q) * CH]], axis=1
    )


def message_tasks(e, low, width, edges, terms, terms0, msg):
    rows = pl.ds(pl.multiple_of(e * BLOCK + low, BLOCK), width)

    def scalar():
        msg[0, rows, :] += mm(edges[0], terms0[:, 0:CH])

    def carried(k):
        both = mm(edges[0], terms0[:, k * CH : (k + 2) * CH])
        msg[k, rows, :] += both[:, 0:CH]
        msg[k + 1, rows, :] += both[:, CH:]

    def paired(k):
        both = mm(edges[k], pair_terms(terms, k))
        msg[0, rows, :] += both[:, 0:CH]
        msg[k, rows, :] += both[:, CH:]

    return (
        [scalar]
        + [functools.partial(carried, k) for k in range(1, 9, 2)]
        + [functools.partial(paired, k) for k in range(1, 9)]
    )


def pull_tasks(e, low, width, radial, slope, terms, terms0, dmsg, by_r, by_y):
    centre = pl.ds(pl.multiple_of(e * BLOCK + low, BLOCK), width)

    def first():
        grad = mm_t(dmsg[centre, :], terms0[...]).astype(BF16)
        total = None
        for m in range(4):
            sl = slice(m * CH, (m + 1) * CH)
            part = slope[:, sl] * grad[:, sl]
            total = part if total is None else total + part
        by_r[0, 0:width, :] = total

    def order(k):
        lhs = jnp.concatenate([dmsg[centre, 0:CH], dmsg[centre, k * CH : (k + 1) * CH]], axis=1)
        grad = mm_t(lhs, pair_terms(terms, k)).astype(BF16)
        total_r = None
        total_y = None
        for m in range(4):
            sl = slice(m * CH, (m + 1) * CH)
            part_r = slope[:, sl] * grad[:, sl]
            part_y = radial[:, sl] * grad[:, sl]
            total_r = part_r if total_r is None else total_r + part_r
            total_y = part_y if total_y is None else total_y + part_y
        by_r[k, 0:width, :] = total_r
        by_y[k, 0:width, :] = total_y

    return [first] + [functools.partial(order, k) for k in range(1, 9)]


def force_tasks(e, low, width, by_r, by_y, pos_i, pos_j, keep, cols, nbr_out):
    state = {"tot": [jnp.zeros((CHUNK, CH), F32) for _ in range(3)]}
    lane = lax.broadcasted_iota(jnp.int32, (CHUNK, CH), 1)

    def task(row0):
        rows = slice(row0 - low, row0 - low + CHUNK)
        dx, dy, dz, x2, y2, z2 = geometry(e, row0, pos_i, pos_j, keep)
        ys = harmonics(dx, dy, dz, x2, y2, z2)
        radial_sum = by_r[0, rows, :].astype(F32)
        for k in range(1, 9):
            radial_sum += ys[k] * by_r[k, rows, :].astype(F32)
        radial_sum *= 2.0
        gy = [None] + [by_y[k, rows, :].astype(F32) for k in range(1, 9)]
        along = radial_sum - gy[6]
        parts = (
            dx * along + gy[1] + ROOT_THREE * (dy * gy[4] + dz * gy[7] + dx * gy[8]),
            dy * along + gy[2] + ROOT_THREE * (dx * gy[4] + dz * gy[5] - dy * gy[8]),
            dz * (radial_sum + 2.0 * gy[6]) + gy[3] + ROOT_THREE * (dy * gy[5] + dx * gy[7]),
        )
        state["tot"] = [a + b for a, b in zip(state["tot"], parts)]
        sums = [jnp.sum(p, axis=1, keepdims=True) for p in parts]
        add = jnp.where(
            lane == 0, sums[0], jnp.where(lane == 1, sums[1], jnp.where(lane == 2, sums[2], 0.0))
        )
        at = pl.ds(pl.multiple_of(e * BLOCK + row0, CHUNK), CHUNK)
        cols[at, :] += add

    def finish():
        sub = lax.broadcasted_iota(jnp.int32, (8, CH), 0)
        sums = [jnp.sum(p, axis=0, keepdims=True) for p in state["tot"]]
        nbr_out[e] = jnp.where(
            sub == 0, sums[0], jnp.where(sub == 1, sums[1], jnp.where(sub == 2, sums[2], 0.0))
        )

    return [functools.partial(task, row0) for row0 in range(low, low + width, CHUNK)] + [finish]


def block_kernel(
    keep,
    count,
    arrival,
    live_in,
    received,
    pos_i,
    pos_j,
    gains,
    weights_in,
    mix,
    self_w,
    readout,
    force_out,
    energy_out,
    new_out,
    pick,
    feats,
    nbr_out,
    inbox,
    edges_a,
    edges_b,
    rad_all,
    slope_all,
    terms_a,
    terms_b,
    first_a,
    first_b,
    edges_h,
    slopes_h,
    msg,
    dmsg,
    by_r_a,
    by_r_b,
    by_y_a,
    by_y_b,
    cols,
    weights,
    send_sems,
    recv_sems,
):
    own_blocks = pos_j.shape[0] - 2
    width = 3 * BLOCK
    weights[...] = weights_in[...].astype(BF16)
    inner = lax.axis_size("blk")
    ranks = lax.axis_size("dom") * inner
    me = lax.axis_index("dom") * inner + lax.axis_index("blk")

    def place(rank):
        return (rank // inner, lax.rem(rank, inner))

    after = place(lax.rem(me + 1, ranks))
    before = place(lax.rem(me + ranks - 1, ranks))

    def send(source, target, lane, device):
        return pltpu.make_async_remote_copy(
            src_ref=source,
            dst_ref=target,
            send_sem=send_sems.at[lane],
            recv_sem=recv_sems.at[lane],
            device_id=device,
            device_id_type=pl.DeviceIdType.MESH,
        )

    barrier = pltpu.get_barrier_semaphore()
    for device in (before, after):
        pl.semaphore_signal(barrier, inc=1, device_id=device, device_id_type=pl.DeviceIdType.MESH)

    rows_own = own_blocks * BLOCK
    index = arrival[...]
    slot_of = (index // 6) * 8 + index % 6
    alive = live_in[...]
    for tile in range(received.shape[0] // CH):
        lane_id = lax.broadcasted_iota(jnp.int32, (rows_own, CH), 1) + tile * CH
        pick[:, tile * CH : (tile + 1) * CH] = jnp.where(slot_of == lane_id, alive, 0.0).astype(BF16)
    for low in range(0, 9 * CH, 2 * CH):
        high = min(low + 2 * CH, 9 * CH)
        feats[BLOCK : BLOCK + rows_own, low:high] = mm(pick[...], received[:, low:high]).astype(BF16)

    pl.semaphore_wait(barrier, 2)
    to_before = send(feats.at[BLOCK : 2 * BLOCK], feats.at[BLOCK + rows_own : 2 * BLOCK + rows_own], 0, before)
    to_after = send(feats.at[rows_own : BLOCK + rows_own], feats.at[0:BLOCK], 1, after)
    to_before.start()
    to_after.start()
    edge_bufs = (edges_a, edges_b)
    term_bufs, first_bufs = (terms_a, terms_b), (first_a, first_b)
    sums_bufs = ((by_r_a, by_y_a), (by_r_b, by_y_b))

    def own_edges(b, buf):
        def put_edge(k, rows, cols_, value):
            buf[k, rows, cols_] = value
            if k == 0:
                rad_all[b, rows, cols_] = value

        def put_slope(rows, cols_, value):
            slope_all[b, rows, cols_] = value

        return edge_tasks(b + 1, 0, width, pos_i, pos_j, keep, put_edge, put_slope)

    msg[...] = jnp.zeros_like(msg)
    cols[...] = jnp.zeros_like(cols)
    dmsg[...] = jnp.zeros_like(dmsg)
    last = own_blocks - 1
    mingle(own_edges(0, edges_a), term_tasks(1, feats, weights, terms_a, first_a))

    def forward(i, carry):
        for half in range(2):
            b = i * 2 + half
            ahead = jnp.minimum(b + 1, last)
            mingle(
                message_tasks(b + 1, 0, width, edge_bufs[half], term_bufs[half], first_bufs[half], msg),
                own_edges(ahead, edge_bufs[1 - half]),
                term_tasks(ahead + 1, feats, weights, term_bufs[1 - half], first_bufs[1 - half]),
            )
        return carry

    lax.fori_loop(0, own_blocks // 2, forward, 0)

    to_before.wait()
    to_after.wait()
    halo = ((0, 2 * BLOCK), (own_blocks + 1, 0))
    for side, (e, low) in enumerate(halo):
        def put_edge(k, rows, cols_, value):
            edges_h[side, k, rows, cols_] = value

        def put_slope(rows, cols_, value):
            slopes_h[side, rows, cols_] = value

        mingle(
            edge_tasks(e, low, BLOCK, pos_i, pos_j, keep, put_edge, put_slope),
            term_tasks(e, feats, weights, term_bufs[side], first_bufs[side]),
        )
    for side, (e, low) in enumerate(halo):
        mingle(
            message_tasks(e, low, BLOCK, edges_h.at[side], term_bufs[side], first_bufs[side], msg)
        )

    size = 2 * BLOCK

    def atoms(i, carry):
        rows = pl.ds(pl.multiple_of(i * size + 2 * BLOCK, size), size)
        own = pl.ds(pl.multiple_of(i * size, size), size)
        ext = pl.ds(pl.multiple_of(i * size + BLOCK, BLOCK), size)
        slot = lax.broadcasted_iota(jnp.int32, (BLOCK, 1), 0)
        live = jnp.concatenate(
            [(slot < count[2 * i + step]).astype(F32) for step in range(2)], axis=0
        )
        m = [msg[k, rows, :] for k in range(9)]
        first = m[1] * m[1] + m[2] * m[2] + m[3] * m[3]
        second = m[4] * m[4] + m[5] * m[5] + m[6] * m[6] + m[7] * m[7] + m[8] * m[8]
        g0, g1, g2 = (gains[own, l * CH : (l + 1) * CH] for l in range(3))
        basis = m[0] + g0 * (m[0] * m[0]) + g1 * first + g2 * second
        mixed = mm(basis.astype(BF16), mix[...]) + mm(feats[ext, 0:CH], self_w[...])
        new_out[own, :] = (mixed * live).astype(BF16)
        gate = 1.0 / (1.0 + jnp.exp(-mixed))
        value = mixed * gate
        energy = live * jnp.sum(readout[...] * value, axis=1, keepdims=True)
        slope = live * readout[...] * (gate + value * (1.0 - gate))
        dbasis = mm_t(slope.astype(BF16), mix[...]).astype(BF16).astype(F32)
        dmsg[rows, 0:CH] = (dbasis * (1.0 + 2.0 * g0 * m[0])).astype(BF16)
        for k in range(1, 9):
            gain = g1 if k < 4 else g2
            dmsg[rows, k * CH : (k + 1) * CH] = (2.0 * dbasis * gain * m[k]).astype(BF16)
        lane = lax.broadcasted_iota(jnp.int32, (size, CH), 1)
        cols[rows, :] = jnp.where(lane == 3, energy, 0.0)
        return carry

    lax.fori_loop(0, own_blocks // 2, atoms, 0)

    for side, (e, low) in enumerate(halo):
        mingle(
            pull_tasks(
                e, low, BLOCK, edges_h.at[side, 0], slopes_h.at[side], term_bufs[side],
                first_bufs[side], dmsg, *sums_bufs[side],
            )
        )
    for side, (e, low) in enumerate(halo):
        mingle(force_tasks(e, low, BLOCK, *sums_bufs[side], pos_i, pos_j, keep, cols, nbr_out))
    force_before = send(nbr_out.at[0], inbox.at[0], 2, before)
    force_after = send(nbr_out.at[own_blocks + 1], inbox.at[1], 3, after)
    force_before.start()
    force_after.start()
    mingle(term_tasks(1, feats, weights, terms_a, first_a))

    def pull(b, half):
        return pull_tasks(
            b + 1, 0, width, rad_all.at[b], slope_all.at[b], term_bufs[half], first_bufs[half],
            dmsg, *sums_bufs[half],
        )

    def ahead_terms(b, half):
        return term_tasks(b + 1, feats, weights, term_bufs[half], first_bufs[half])

    def force(b, half):
        return force_tasks(
            b + 1, 0, width, *sums_bufs[half], pos_i, pos_j, keep, cols, nbr_out
        )

    mingle(pull(0, 0), ahead_terms(1, 1))

    def backward(i, carry):
        b = i * 2 + 1
        mingle(pull(b, 1), force(b - 1, 0), ahead_terms(b + 1, 0))
        mingle(pull(b + 1, 0), force(b, 1), ahead_terms(jnp.minimum(b + 2, last), 1))
        return carry

    lax.fori_loop(0, own_blocks // 2 - 1, backward, 0)
    mingle(pull(last, 1), force(last - 1, 0))
    mingle(force(last, 1))
    force_before.wait()
    force_after.wait()
    nbr_out[1] += inbox[1]
    nbr_out[own_blocks] += inbox[0]
    half_lane = lax.broadcasted_iota(jnp.int32, (8, CH), 1) < BLOCK
    for i in range(own_blocks // 2):
        lanes = slice(i * CH, (i + 1) * CH)
        flat = jnp.transpose(cols[2 * BLOCK + i * CH : 2 * BLOCK + (i + 1) * CH, :])[0:8, :]
        even, odd_ = nbr_out[2 * i + 1], nbr_out[2 * i + 2]
        even = even + pltpu.roll(even, BLOCK, 1)
        odd_ = odd_ + pltpu.roll(odd_, BLOCK, 1)
        total = flat - jnp.where(half_lane, even, odd_)
        force_out[:, lanes] = total[0:3, :]
        energy_out[:, lanes] = total[3:4, :]


def block_stage(
    keep, count, arrival, live, received, pos_i, pos_j, gains, weights, mix, self_w, readout
):
    ext_blocks = pos_j.shape[0]
    own_rows = (ext_blocks - 2) * BLOCK
    pad_rows = pos_i.shape[0]
    vmem = pl.BlockSpec(memory_space=pltpu.VMEM)
    smem = pl.BlockSpec(memory_space=pltpu.SMEM)
    width, depth = 3 * BLOCK, NB * BLOCK
    return pl.pallas_call(
        block_kernel,
        out_shape=(
            jax.ShapeDtypeStruct((3, own_rows), F32),
            jax.ShapeDtypeStruct((1, own_rows), F32),
            jax.ShapeDtypeStruct((own_rows, CH), BF16),
        ),
        in_specs=[smem, smem] + [vmem] * 10,
        out_specs=(vmem, vmem, vmem),
        scratch_shapes=[
            pltpu.VMEM((own_rows, received.shape[0]), BF16),
            pltpu.VMEM((own_rows + 2 * BLOCK, 9 * CH), BF16),
            pltpu.VMEM((ext_blocks, 8, CH), F32),
            pltpu.VMEM((2, 8, CH), F32),
            pltpu.VMEM((9, width, depth), BF16),
            pltpu.VMEM((9, width, depth), BF16),
            pltpu.VMEM((ext_blocks - 2, width, depth), BF16),
            pltpu.VMEM((ext_blocks - 2, width, depth), BF16),
            pltpu.VMEM((depth, 10 * CH), BF16),
            pltpu.VMEM((depth, 10 * CH), BF16),
            pltpu.VMEM((depth, 9 * CH), BF16),
            pltpu.VMEM((depth, 9 * CH), BF16),
            pltpu.VMEM((2, 9, BLOCK, depth), BF16),
            pltpu.VMEM((2, BLOCK, depth), BF16),
            pltpu.VMEM((9, pad_rows, CH), F32),
            pltpu.VMEM((pad_rows, 9 * CH), BF16),
            pltpu.VMEM((9, width, CH), BF16),
            pltpu.VMEM((9, width, CH), BF16),
            pltpu.VMEM((9, width, CH), BF16),
            pltpu.VMEM((9, width, CH), BF16),
            pltpu.VMEM((pad_rows, CH), F32),
            pltpu.VMEM((NB, 7, CH), BF16),
            pltpu.SemaphoreType.DMA((4,)),
            pltpu.SemaphoreType.DMA((4,)),
        ],
        compiler_params=pltpu.CompilerParams(
            vmem_limit_bytes=50 * 1024 * 1024, collective_id=0, has_side_effects=True
        ),
        name="block_stage",
    )(keep, count, arrival, live, received, pos_i, pos_j, gains, weights, mix, self_w, readout)


def ring_pairs(axes):
    count = math.prod(lax.axis_size(axis) for axis in axes)
    forward = [(i, i + 1) for i in range(count - 1)]
    backward = [(target, source) for source, target in forward]
    return forward, backward


def per_device(
    features_domain,
    arrival,
    positions,
    species,
    block_count,
    pair_block,
    radial_weights,
    species_weights,
    mix_weight,
    self_weight,
    readout,
):
    axes = ("dom", "blk")
    devices = lax.axis_size(axes)
    atom_rows, feature_cols = features_domain.shape
    piece = atom_rows // devices
    blocks = atom_rows // BLOCK
    forward, backward = ring_pairs(axes)

    parcels = jnp.pad(
        features_domain.reshape(devices, piece, feature_cols), ((0, 0), (0, 8 - piece), (0, 0))
    )
    received = lax.all_to_all(parcels, axes, split_axis=0, concat_axis=0, tiled=True)
    received = received.reshape(devices * 8, feature_cols)

    coords = positions.T
    low = lax.ppermute(coords[:, atom_rows - BLOCK :], axes, forward)
    high = lax.ppermute(coords[:, :BLOCK], axes, backward)
    coords_ext = jnp.concatenate([low, coords, high], axis=1)
    pos_i = jnp.pad(coords_ext, ((0, 5), (BLOCK, BLOCK))).T
    by_block = coords_ext.reshape(3, blocks + 2, BLOCK).transpose(1, 0, 2)
    pos_j = jnp.pad(jnp.concatenate([by_block, by_block], axis=2), ((0, 0), (0, 5), (0, 0)))
    listed = jnp.pad((pair_block >= 0).astype(F32), ((2, 2), (0, 0)))
    keep = jnp.stack(
        [listed[0 : blocks + 2, 2], listed[1 : blocks + 3, 1], listed[2 : blocks + 4, 0]], axis=1
    ).reshape(-1)
    live = (jnp.arange(BLOCK, dtype=jnp.int32)[None, :] < block_count[:, None]).astype(F32)
    total = species_weights.shape[0]
    one_hot = (species[:, None] == jnp.arange(total, dtype=jnp.int32)[None, :]).astype(F32)
    gains = jnp.dot(one_hot, species_weights.reshape(total, -1), precision=lax.Precision.HIGHEST)

    forces, energies, new_rows = block_stage(
        keep,
        block_count,
        arrival[:, None],
        live.reshape(atom_rows, 1),
        received,
        pos_i,
        pos_j,
        gains,
        radial_weights,
        mix_weight,
        self_weight,
        readout[None, :],
    )
    return (energies.reshape(atom_rows), forces.T, new_rows)


def solution(mesh):
    placed = (
        P(("dom", "blk"), None),
        P(("dom", "blk")),
        P(("dom", "blk"), None),
        P(("dom", "blk")),
        P(("dom", "blk")),
        P(("dom", "blk"), None),
        P(),
        P(),
        P(),
        P(),
        P(),
    )
    return jax.shard_map(
        per_device,
        mesh=mesh,
        in_specs=placed,
        out_specs=(P(("dom", "blk")), P(("dom", "blk"), None), P(("dom", "blk"), None)),
        check_vma=False,
    )
```

time: 136 us -> 103 us (0.76)
  the two profiles are of different devices: /device:TPU:111 before, /device:TPU:1 now
where the time goes in v2:
time: 103 us
  Pallas kernels  50.7 us (49%)
  waiting for transfers between devices  25.2 us (24%)
  starting transfers between devices  17.4 us (17%)
  local copies, waits for them, and re-layouts  7.07 us (7%)
    pallas_call x1, Pallas kernels, block_stage(): pl.pallas_call(block_kernel, out_shape=(jax.ShapeDtypeStruct((3, own_rows...  50.7 us
    ppermute x1, waiting for transfers between devices, per_device(): low = lax.ppermute(coords[:, atom_rows - BLOCK:], axes, forward)  16.2 us
    all_to_all x1, starting transfers between devices, per_device(): lax.all_to_all(parcels, axes, split_axis=0, concat_axis=0, tiled=True)  11.9 us
    all_to_all x1, waiting for transfers between devices, per_device(): lax.all_to_all(parcels, axes, split_axis=0, concat_axis=0, tiled=True)  5.68 us
    ppermute x1, starting transfers between devices, per_device(): low = lax.ppermute(coords[:, atom_rows - BLOCK:], axes, forward)  3.53 us
    ppermute x1, waiting for transfers between devices, per_device(): high = lax.ppermute(coords[:, :BLOCK], axes, backward)  3.34 us
    reshape x1, local copies, waits for them, and re-layouts, per_device(): features_domain.reshape(devices, piece, feature_cols)  2.55 us
  transfers between devices with their start and end apart: 3, of which 3 were waited for; matrix products, arithmetic and copies ran while one was open for 2% of the time, Pallas kernels for 0%

profile of v2, /device:TPU:1, one launch (start us, length us, event | category | flops | bytes accessed | tf_op | source)
XLA Modules:
  0.0 102.8 jit_solution(16385256485691180223)
XLA Ops:
  0.6 2.5 %reshape.55 = bf16[128,6,1152]{2,1,0:T(8,128)(2,1)S(1)} reshape(bf16[768,1152]{1,0:T(8,128)(2,1)} %param.11) | data formatting | bytes 3538944 | tf_op jit(solution)/shard_map/reshape | solution.py:545
  3.2 1.9 %pad.21 = bf16[128,8,1152]{2,1,0:T(8,128)(2,1)} pad(bf16[128,6,1152]{2,1,0:T(8,128)(2,1)S(1)} %reshape.55, bf16[]{:T(256)} %constant.7.clone.1), padding=0_0x0_2x0_0 | pad | bytes 4128770 | tf_op jit(solution)/shard_map/jit(_pad)/pad | solution.py:544
  5.1 0.0 copy-start.6
  5.1 0.0 copy-start.4
  5.1 0.0 copy-start.9
  5.1 0.0 copy-start.2
  5.1 0.0 copy-start.7
  5.1 11.9 %all-to-all-start = ((bf16[128,8,1152]{2,1,0:T(8,128)(2,1)}), bf16[128,8,1152]{2,1,0:T(8,128)(2,1)}, u32[]{:S(2)}, u32[]{:S(2)}) async-start(bf16[128,8,1152]{2,1,0:T(8,128)(2,1)} %pad.21), calls=%async_computation | async-start | bytes 4718592 | tf_op jit(solution)/shard_map/all_to_all | solution.py:547
  17.0 0.0 copy-start.8
  17.0 0.0 copy-start.5
  17.0 0.0 copy-done.6
  17.0 0.1 fusion.3
  17.1 3.5 %collective-permute-start = (f32[3,64]{1,0:T(4,128)S(1)}, f32[3,64]{1,0:T(4,128)S(1)}, u32[]{:S(2)}, u32[]{:S(2)}) collective-permute-start(f32[3,64]{1,0:T(4,128)S(1)} %get-tuple-element.9), channel_id=1, source_target_pairs={{0,1},{1,2},{2,3},{3,4},{4,5},{5,6},{6,7},{7,8},{8,9},{9,10},{10,1... | collective-permute-start | bytes 2312 | tf_op jit(solution)/shard_map/ppermute | solution.py:551
  20.6 1.9 %collective-permute-start.1 = (f32[3,64]{1,0:T(4,128)S(1)}, f32[3,64]{1,0:T(4,128)S(1)}, u32[]{:S(2)}, u32[]{:S(2)}) collective-permute-start(f32[3,64]{1,0:T(4,128)S(1)} %get-tuple-element.10), channel_id=1, source_target_pairs={{1,0},{2,1},{3,2},{4,3},{5,4},{6,5},{7,6},{8,7},{9,8},{10,9},{11,1... | collective-permute-start | bytes 2312 | tf_op jit(solution)/shard_map/ppermute | solution.py:552
  22.6 0.0 copy-done.4
  22.6 0.1 copy.28
  22.7 0.0 copy-start
  22.7 0.0 copy-start.1
  22.7 0.0 copy-start.3
  22.8 0.0 copy-done.9
  22.8 0.1 pad_convert_fusion
  22.9 0.1 fusion.4
  23.0 0.0 copy-done.2
  23.0 0.1 fusion.2
  23.0 0.0 copy-done.7
  23.0 0.7 fusion.gains
  23.7 0.1 copy.25
  23.8 0.1 reshape.54.keep
  23.9 0.3 reshape.61.live_in
  24.3 0.0 copy-done.8
  24.3 0.2 broadcast_in_dim.12.arrival
  24.4 0.0 copy-done.5
  24.5 16.2 %collective-permute-done = f32[3,64]{1,0:T(4,128)S(1)} collective-permute-done((f32[3,64]{1,0:T(4,128)S(1)}, f32[3,64]{1,0:T(4,128)S(1)}, u32[]{:S(2)}, u32[]{:S(2)}) %collective-permute-start) | collective-permute-done | bytes 800 | tf_op jit(solution)/shard_map/ppermute | solution.py:551
  40.6 3.3 %collective-permute-done.1 = f32[3,64]{1,0:T(4,128)S(1)} collective-permute-done((f32[3,64]{1,0:T(4,128)S(1)}, f32[3,64]{1,0:T(4,128)S(1)}, u32[]{:S(2)}, u32[]{:S(2)}) %collective-permute-start.1) | collective-permute-done | bytes 800 | tf_op jit(solution)/shard_map/ppermute | solution.py:552
  44.0 0.1 pad_maximum_fusion
  44.0 0.2 copy.26
  44.3 0.1 reshape.57
  44.4 0.1 select_maximum_fusion.pos_j
  44.5 5.7 %all-to-all-done = bf16[128,8,1152]{2,1,0:T(8,128)(2,1)} async-done(((bf16[128,8,1152]{2,1,0:T(8,128)(2,1)}), bf16[128,8,1152]{2,1,0:T(8,128)(2,1)}, u32[]{:S(2)}, u32[]{:S(2)}) %all-to-all-start) | async-done | bytes 2359328 | tf_op jit(solution)/shard_map/all_to_all | solution.py:547
  50.2 0.0 copy-done
  50.2 0.0 copy-done.1
  50.2 0.0 copy-done.3
  50.2 50.7 %block_stage.1 = (f32[3,768]{1,0:T(4,128)S(1)}, f32[1,768]{1,0:T(1,128)S(1)}, bf16[768,128]{1,0:T(8,128)(2,1)S(1)}) custom-call(f32[42]{0:T(128)S(1)} %reshape.54.keep, s32[12]{0:T(128)S(1)} %copy-done.2, s32[768,1]{1,0:T(8,128)S(1)} %broadcast_in_dim.12.arrival, f32[768,1]{1,0:T(8,128)S(1)} %reshape.61.live_in, bf16[1024,1152]{1,0:T(8,128)(2,1)} %bitcast.received, ...), custom_call_target="tpu_custom_call" | custom-call | tf_op jit(solution)/shard_map/block_stage/pallas_call | solution.py:475
  100.9 0.6 reduce
  101.5 0.6 copy.37
  102.1 0.7 copy.38
  (7 shorter events, 0.1 us)
Async XLA Ops:
  5.1 12.0 %copy-start.6 = (f32[768,3]{0,1:T(4,128)S(1)}, f32[768,3]{0,1:T(4,128)}, u32[]{:S(2)}) copy-start(f32[768,3]{0,1:T(4,128)} %param.13) | copy-start | bytes 27652
  5.1 17.5 %copy-start.4 = (f32[89,3,128]{2,0,1:T(8,128)S(1)}, f32[89,3,128]{2,0,1:T(8,128)}, u32[]{:S(2)}) copy-start(f32[89,3,128]{2,0,1:T(8,128)} %param.18) | copy-start | bytes 410116
  5.1 17.7 %copy-start.9 = (s32[12,3]{0,1:T(4,128)S(1)}, s32[12,3]{0,1:T(4,128)}, u32[]{:S(2)}) copy-start(s32[12,3]{0,1:T(4,128)} %param.16) | copy-start | bytes 436
  5.1 17.9 %copy-start.2 = (s32[12]{0:T(128)S(1)}, s32[12]{0:T(128)}, u32[]{:S(2)}) copy-start(s32[12]{0:T(128)} %count.1) | copy-start | bytes 148
  5.1 18.0 %copy-start.7 = (s32[768]{0:T(1024)S(1)}, s32[768]{0:T(1024)}, u32[]{:S(2)}) copy-start(s32[768]{0:T(1024)} %param.14) | copy-start | bytes 9220
  5.1 45.1 %all-to-all-start = ((bf16[128,8,1152]{2,1,0:T(8,128)(2,1)}), bf16[128,8,1152]{2,1,0:T(8,128)(2,1)}, u32[]{:S(2)}, u32[]{:S(2)}) async-start(bf16[128,8,1152]{2,1,0:T(8,128)(2,1)} %pad.21), calls=%async_computation | async-start | bytes 4718592 | tf_op jit(solution)/shard_map/all_to_all | solution.py:547
  17.0 7.3 %copy-start.8 = (s32[768]{0:T(1024)S(1)}, s32[768]{0:T(1024)}, u32[]{:S(2)}) copy-start(s32[768]{0:T(1024)} %param.12) | copy-start | bytes 9220
  17.0 7.4 %copy-start.5 = (f32[8,7,128]{2,0,1:T(8,128)S(1)}, f32[8,7,128]{2,0,1:T(8,128)}, u32[]{:S(2)}) copy-start(f32[8,7,128]{2,0,1:T(8,128)} %param.17) | copy-start | bytes 86020
  17.1 23.5 %collective-permute-start = (f32[3,64]{1,0:T(4,128)S(1)}, f32[3,64]{1,0:T(4,128)S(1)}, u32[]{:S(2)}, u32[]{:S(2)}) collective-permute-start(f32[3,64]{1,0:T(4,128)S(1)} %get-tuple-element.9), channel_id=1, source_target_pairs={{0,1},{1,2},{2,3},{3,4},{4,5},{5,6},{6,7},{7,8},{8,9},{9,10},{10,1... | collective-permute-start | bytes 2312 | tf_op jit(solution)/shard_map/ppermute | solution.py:551
  20.6 23.3 %collective-permute-start.1 = (f32[3,64]{1,0:T(4,128)S(1)}, f32[3,64]{1,0:T(4,128)S(1)}, u32[]{:S(2)}, u32[]{:S(2)}) collective-permute-start(f32[3,64]{1,0:T(4,128)S(1)} %get-tuple-element.10), channel_id=1, source_target_pairs={{1,0},{2,1},{3,2},{4,3},{5,4},{6,5},{7,6},{8,7},{9,8},{10,9},{11,1... | collective-permute-start | bytes 2312 | tf_op jit(solution)/shard_map/ppermute | solution.py:552
  22.7 27.5 %copy-start = (bf16[128,128]{1,0:T(8,128)(2,1)S(1)}, bf16[128,128]{1,0:T(8,128)(2,1)}, u32[]{:S(2)}) copy-start(bf16[128,128]{1,0:T(8,128)(2,1)} %mix.1) | copy-start | bytes 98308
  22.7 27.5 %copy-start.1 = (bf16[128,128]{1,0:T(8,128)(2,1)S(1)}, bf16[128,128]{1,0:T(8,128)(2,1)}, u32[]{:S(2)}) copy-start(bf16[128,128]{1,0:T(8,128)(2,1)} %self_w.1) | copy-start | bytes 98308
  22.7 27.5 %copy-start.3 = (f32[128]{0:T(128)S(1)}, f32[128]{0:T(128)}, u32[]{:S(2)}) copy-start(f32[128]{0:T(128)} %param.21) | copy-start | bytes 1540

commit v3 on v2

--- a/solution.py
+++ b/solution.py
@@ -17,6 +17,7 @@
 LIFT_PATH = (-1, 1, 1, 1, 2, 2, 2, 2, 2)
 CHUNK = 16
 NB = 8
+PIECE = 6
 F32 = jnp.float32
 BF16 = jnp.bfloat16
 
@@ -238,6 +239,44 @@
     return [functools.partial(task, row0) for row0 in range(low, low + width, CHUNK)] + [finish]
 
 
+def fill_pick(pick, slot_of, alive, width):
+    for tile in range(width // CH):
+        lane_id = lax.broadcasted_iota(jnp.int32, (slot_of.shape[0], CH), 1) + tile * CH
+        pick[:, tile * CH : (tile + 1) * CH] = jnp.where(slot_of == lane_id, alive, 0.0).astype(BF16)
+
+
+def pack_kernel(rows_in, out):
+    group, source = 256, 256 // 8 * PIECE
+    row = lax.broadcasted_iota(jnp.int32, (group, source), 0)
+    col = lax.broadcasted_iota(jnp.int32, (group, source), 1)
+    parcel, within = row // 8, row % 8
+    plain = ((within < PIECE) & (col == parcel * PIECE + within)).astype(F32).astype(BF16)
+    last = lax.broadcasted_iota(jnp.int32, (group, CH), 0) % 8 == PIECE + 1
+    for t in range(7):
+        cols = slice(t * CH, (t + 1) * CH)
+        if t < PIECE:
+            extra = ((within >= PIECE) & (col == parcel * PIECE + t)).astype(F32).astype(BF16)
+        for g in range(out.shape[0] // group):
+            at = slice(g * source, (g + 1) * source)
+            value = mm(plain, rows_in[at, cols])
+            if t < PIECE:
+                both = mm(extra, rows_in[at, 7 * CH : 9 * CH])
+                value += jnp.where(last, both[:, CH:], both[:, 0:CH])
+            out[g * group : (g + 1) * group, cols] = value.astype(BF16)
+
+
+def pack_stage(rows_in):
+    vmem = pl.BlockSpec(memory_space=pltpu.VMEM)
+    return pl.pallas_call(
+        pack_kernel,
+        out_shape=jax.ShapeDtypeStruct((rows_in.shape[0] // PIECE * 8, 7 * CH), BF16),
+        in_specs=[vmem],
+        out_specs=vmem,
+        compiler_params=pltpu.CompilerParams(vmem_limit_bytes=16 * 1024 * 1024),
+        name="pack_stage",
+    )(rows_in)
+
+
 def block_kernel(
     keep,
     count,
@@ -255,6 +294,7 @@
     energy_out,
     new_out,
     pick,
+    sorted_rows,
     feats,
     nbr_out,
     inbox,
@@ -308,14 +348,30 @@
 
     rows_own = own_blocks * BLOCK
     index = arrival[...]
-    slot_of = (index // 6) * 8 + index % 6
+    parcel = index // PIECE
+    within = index - parcel * PIECE
     alive = live_in[...]
-    for tile in range(received.shape[0] // CH):
-        lane_id = lax.broadcasted_iota(jnp.int32, (rows_own, CH), 1) + tile * CH
-        pick[:, tile * CH : (tile + 1) * CH] = jnp.where(slot_of == lane_id, alive, 0.0).astype(BF16)
-    for low in range(0, 9 * CH, 2 * CH):
-        high = min(low + 2 * CH, 9 * CH)
-        feats[BLOCK : BLOCK + rows_own, low:high] = mm(pick[...], received[:, low:high]).astype(BF16)
+    own_feats = slice(BLOCK, BLOCK + rows_own)
+    senders = received.shape[0] // 8
+    slot_of = within * senders + parcel
+    fill_pick(pick, slot_of, alive, PIECE * senders)
+    sub_id = lax.broadcasted_iota(jnp.int32, (senders, received.shape[0]), 0)
+    row_id = lax.broadcasted_iota(jnp.int32, (senders, received.shape[0]), 1)
+    for extra in range(2):
+        take = (row_id == sub_id * 8 + (PIECE + extra)).astype(F32).astype(BF16)
+        for low in range(0, PIECE * CH, 2 * CH):
+            both = mm(take, received[:, low : low + 2 * CH]).astype(BF16)
+            for step in range(2):
+                r = low // CH + step
+                sorted_rows[r * senders : (r + 1) * senders, extra * CH : (extra + 1) * CH] = both[
+                    :, step * CH : (step + 1) * CH
+                ]
+    feats[own_feats, 7 * CH : 9 * CH] = mm(pick[:, 0 : PIECE * senders], sorted_rows[...]).astype(BF16)
+    slot_of = parcel * 8 + within
+    fill_pick(pick, slot_of, alive, received.shape[0])
+    for low in range(0, 7 * CH, 2 * CH):
+        high = min(low + 2 * CH, 7 * CH)
+        feats[own_feats, low:high] = mm(pick[...], received[:, low:high]).astype(BF16)
 
     pl.semaphore_wait(barrier, 2)
     to_before = send(feats.at[BLOCK : 2 * BLOCK], feats.at[BLOCK + rows_own : 2 * BLOCK + rows_own], 0, before)
@@ -483,6 +539,7 @@
         out_specs=(vmem, vmem, vmem),
         scratch_shapes=[
             pltpu.VMEM((own_rows, received.shape[0]), BF16),
+            pltpu.VMEM((PIECE * received.shape[0] // 8, 2 * CH), BF16),
             pltpu.VMEM((own_rows + 2 * BLOCK, 9 * CH), BF16),
             pltpu.VMEM((ext_blocks, 8, CH), F32),
             pltpu.VMEM((2, 8, CH), F32),
@@ -537,15 +594,12 @@
     axes = ("dom", "blk")
     devices = lax.axis_size(axes)
     atom_rows, feature_cols = features_domain.shape
-    piece = atom_rows // devices
     blocks = atom_rows // BLOCK
     forward, backward = ring_pairs(axes)
 
-    parcels = jnp.pad(
-        features_domain.reshape(devices, piece, feature_cols), ((0, 0), (0, 8 - piece), (0, 0))
-    )
+    parcels = pack_stage(features_domain).reshape(devices, 8, 7 * CH)
     received = lax.all_to_all(parcels, axes, split_axis=0, concat_axis=0, tiled=True)
-    received = received.reshape(devices * 8, feature_cols)
+    received = received.reshape(devices * 8, 7 * CH)
 
     coords = positions.T
     low = lax.ppermute(coords[:, atom_rows - BLOCK :], axes, forward)

time: 103 us -> 96.3 us (0.935)
  waiting for transfers between devices: 25.2 us -> 19.7 us
  local copies, waits for them, and re-layouts: 7.07 us -> 4.12 us
  Pallas kernels: 50.7 us -> 52.4 us
    ppermute x1, waiting for transfers between devices: 16.2 us -> 10.6 us  [per_device(): low = lax.ppermute(coords[:, atom_rows - BLOCK:], axes, forward)]
    pallas_call x0 -> x1, Pallas kernels: none -> 3.2 us  [pack_stage(): pl.pallas_call(pack_kernel, out_shape=jax.ShapeDtypeStruct((rows_in.shape...]
    reshape x1 -> x0, local copies, waits for them, and re-layouts: 2.55 us -> none  [per_device(): features_domain.reshape(devices, piece, feature_cols)]
    pad x1 -> x0, local copies, waits for them, and re-layouts: 1.87 us -> none  [per_device(): jnp.pad(features_domain.reshape(devices, piece, feature_cols), ((0, 0), (...]
    pallas_call x1, Pallas kernels: 50.7 us -> 49.1 us  [block_stage(): pl.pallas_call(block_kernel, out_shape=(jax.ShapeDtypeStruct((3, own_rows...]
    unnamed x26 -> x28, local copies, waits for them, and re-layouts: 1.48 us -> 2.95 us
where the time goes in v3:
time: 96.3 us; the launch traced here: 96 us
  Pallas kernels  52.4 us (54%)
  waiting for transfers between devices  19.7 us (20%)
  starting transfers between devices  17.4 us (18%)
  local copies, waits for them, and re-layouts  4.12 us (4%)
    pallas_call x1, Pallas kernels, block_stage(): pl.pallas_call(block_kernel, out_shape=(jax.ShapeDtypeStruct((3, own_rows...  49.1 us
    all_to_all x1, starting transfers between devices, per_device(): lax.all_to_all(parcels, axes, split_axis=0, concat_axis=0, tiled=True)  11.9 us
    ppermute x1, waiting for transfers between devices, per_device(): low = lax.ppermute(coords[:, atom_rows - BLOCK:], axes, forward)  10.6 us
    all_to_all x1, waiting for transfers between devices, per_device(): lax.all_to_all(parcels, axes, split_axis=0, concat_axis=0, tiled=True)  5.8 us
    ppermute x1, starting transfers between devices, per_device(): low = lax.ppermute(coords[:, atom_rows - BLOCK:], axes, forward)  3.53 us
    ppermute x1, waiting for transfers between devices, per_device(): high = lax.ppermute(coords[:, :BLOCK], axes, backward)  3.34 us
    pallas_call x1, Pallas kernels, pack_stage(): pl.pallas_call(pack_kernel, out_shape=jax.ShapeDtypeStruct((rows_in.shape...  3.2 us
    unnamed x28, local copies, waits for them, and re-layouts  2.95 us
  transfers between devices with their start and end apart: 3, of which 3 were waited for; matrix products, arithmetic and copies ran while one was open for 2% of the time, Pallas kernels for 0%

profile of v3, /device:TPU:1, one launch (start us, length us, event | category | flops | bytes accessed | tf_op | source)
XLA Modules:
  0.0 96.0 jit_solution(5498217496987196748)
XLA Ops:
  0.6 0.0 copy-start
  0.6 1.5 %copy-done = bf16[768,1152]{1,0:T(8,128)(2,1)S(1)} copy-done((bf16[768,1152]{1,0:T(8,128)(2,1)S(1)}, bf16[768,1152]{1,0:T(8,128)(2,1)}, u32[]{:S(2)}) %copy-start) | copy-done | bytes 1769496
  2.1 3.2 %pack_stage.1 = bf16[1024,896]{1,0:T(8,128)(2,1)} custom-call(bf16[768,1152]{1,0:T(8,128)(2,1)S(1)} %copy-done), custom_call_target="tpu_custom_call" | custom-call | tf_op jit(solution)/shard_map/pack_stage/pallas_call | solution.py:270
  5.3 0.0 copy-start.7
  5.3 0.0 copy-start.5
  5.3 0.0 copy-start.10
  5.3 0.0 copy-start.3
  5.3 0.0 copy-start.8
  5.3 11.9 %all-to-all-start = ((bf16[128,8,896]{2,1,0:T(8,128)(2,1)}), bf16[128,8,896]{2,1,0:T(8,128)(2,1)}, u32[]{:S(2)}, u32[]{:S(2)}) async-start(bf16[128,8,896]{2,1,0:T(8,128)(2,1)} %bitcast), calls=%async_computation | async-start | bytes 3670016 | tf_op jit(solution)/shard_map/all_to_all | solution.py:601
  17.2 0.0 copy-start.9
  17.3 0.0 copy-start.6
  17.3 0.0 copy-done.7
  17.3 0.1 fusion.3
  17.4 3.5 %collective-permute-start = (f32[3,64]{1,0:T(4,128)S(1)}, f32[3,64]{1,0:T(4,128)S(1)}, u32[]{:S(2)}, u32[]{:S(2)}) collective-permute-start(f32[3,64]{1,0:T(4,128)S(1)} %get-tuple-element.9), channel_id=1, source_target_pairs={{0,1},{1,2},{2,3},{3,4},{4,5},{5,6},{6,7},{7,8},{8,9},{9,10},{10,1... | collective-permute-start | bytes 2312 | tf_op jit(solution)/shard_map/ppermute | solution.py:605
  20.9 1.9 %collective-permute-start.1 = (f32[3,64]{1,0:T(4,128)S(1)}, f32[3,64]{1,0:T(4,128)S(1)}, u32[]{:S(2)}, u32[]{:S(2)}) collective-permute-start(f32[3,64]{1,0:T(4,128)S(1)} %get-tuple-element.10), channel_id=1, source_target_pairs={{1,0},{2,1},{3,2},{4,3},{5,4},{6,5},{7,6},{8,7},{9,8},{10,9},{11,1... | collective-permute-start | bytes 2312 | tf_op jit(solution)/shard_map/ppermute | solution.py:606
  22.8 0.0 copy-done.5
  22.8 0.1 copy.28
  23.0 0.0 copy-done.10
  23.0 0.1 pad_convert_fusion
  23.1 0.1 fusion.4
  23.2 0.0 copy-done.3
  23.2 0.1 fusion.2
  23.2 0.0 copy-done.8
  23.2 0.0 copy-start.1
  23.2 0.0 copy-start.2
  23.3 0.0 copy-start.4
  23.3 0.7 fusion.gains
  24.0 0.1 copy.25
  24.1 0.1 reshape.54.keep
  24.2 0.3 reshape.61.live_in
  24.5 0.0 copy-done.9
  24.5 0.2 broadcast_in_dim.12.arrival
  24.7 0.0 copy-done.6
  24.7 10.6 %collective-permute-done = f32[3,64]{1,0:T(4,128)S(1)} collective-permute-done((f32[3,64]{1,0:T(4,128)S(1)}, f32[3,64]{1,0:T(4,128)S(1)}, u32[]{:S(2)}, u32[]{:S(2)}) %collective-permute-start) | collective-permute-done | bytes 800 | tf_op jit(solution)/shard_map/ppermute | solution.py:605
  35.3 3.3 %collective-permute-done.1 = f32[3,64]{1,0:T(4,128)S(1)} collective-permute-done((f32[3,64]{1,0:T(4,128)S(1)}, f32[3,64]{1,0:T(4,128)S(1)}, u32[]{:S(2)}, u32[]{:S(2)}) %collective-permute-start.1) | collective-permute-done | bytes 800 | tf_op jit(solution)/shard_map/ppermute | solution.py:606
  38.6 0.1 pad_maximum_fusion
  38.7 0.2 copy.26
  38.9 0.1 reshape.57
  39.0 0.1 select_maximum_fusion.pos_j
  39.1 5.8 %all-to-all-done = bf16[128,8,896]{2,1,0:T(8,128)(2,1)} async-done(((bf16[128,8,896]{2,1,0:T(8,128)(2,1)}), bf16[128,8,896]{2,1,0:T(8,128)(2,1)}, u32[]{:S(2)}, u32[]{:S(2)}) %all-to-all-start) | async-done | bytes 1835040 | tf_op jit(solution)/shard_map/all_to_all | solution.py:601
  44.9 0.0 copy-done.1
  44.9 0.0 copy-done.2
  44.9 0.0 copy-done.4
  44.9 49.1 %block_stage.1 = (f32[3,768]{1,0:T(4,128)S(1)}, f32[1,768]{1,0:T(1,128)S(1)}, bf16[768,128]{1,0:T(8,128)(2,1)S(1)}) custom-call(f32[42]{0:T(128)S(1)} %reshape.54.keep, s32[12]{0:T(128)S(1)} %copy-done.3, s32[768,1]{1,0:T(8,128)S(1)} %broadcast_in_dim.12.arrival, f32[768,1]{1,0:T(8,128)S(1)} %reshape.61.live_in, bf16[1024,896]{1,0:T(8,128)(2,1)} %bitcast.1.received, ...), custom_call_target="tpu_custom_call" | custom-call | tf_op jit(solution)/shard_map/block_stage/pallas_call | solution.py:531
  94.1 0.6 reduce
  94.7 0.6 copy.37
  95.3 0.7 copy.38
  (7 shorter events, 0.1 us)
Async XLA Ops:
  0.6 1.5 %copy-start = (bf16[768,1152]{1,0:T(8,128)(2,1)S(1)}, bf16[768,1152]{1,0:T(8,128)(2,1)}, u32[]{:S(2)}) copy-start(bf16[768,1152]{1,0:T(8,128)(2,1)} %rows_in.1) | copy-start | bytes 5308420
  5.3 12.0 %copy-start.7 = (f32[768,3]{0,1:T(4,128)S(1)}, f32[768,3]{0,1:T(4,128)}, u32[]{:S(2)}) copy-start(f32[768,3]{0,1:T(4,128)} %param.13) | copy-start | bytes 27652
  5.3 17.5 %copy-start.5 = (f32[89,3,128]{2,0,1:T(8,128)S(1)}, f32[89,3,128]{2,0,1:T(8,128)}, u32[]{:S(2)}) copy-start(f32[89,3,128]{2,0,1:T(8,128)} %param.18) | copy-start | bytes 410116
  5.3 17.7 %copy-start.10 = (s32[12,3]{0,1:T(4,128)S(1)}, s32[12,3]{0,1:T(4,128)}, u32[]{:S(2)}) copy-start(s32[12,3]{0,1:T(4,128)} %param.16) | copy-start | bytes 436
  5.3 17.9 %copy-start.3 = (s32[12]{0:T(128)S(1)}, s32[12]{0:T(128)}, u32[]{:S(2)}) copy-start(s32[12]{0:T(128)} %count.1) | copy-start | bytes 148
  5.3 17.9 %copy-start.8 = (s32[768]{0:T(1024)S(1)}, s32[768]{0:T(1024)}, u32[]{:S(2)}) copy-start(s32[768]{0:T(1024)} %param.14) | copy-start | bytes 9220
  5.3 39.6 %all-to-all-start = ((bf16[128,8,896]{2,1,0:T(8,128)(2,1)}), bf16[128,8,896]{2,1,0:T(8,128)(2,1)}, u32[]{:S(2)}, u32[]{:S(2)}) async-start(bf16[128,8,896]{2,1,0:T(8,128)(2,1)} %bitcast), calls=%async_computation | async-start | bytes 3670016 | tf_op jit(solution)/shard_map/all_to_all | solution.py:601
  17.2 7.3 %copy-start.9 = (s32[768]{0:T(1024)S(1)}, s32[768]{0:T(1024)}, u32[]{:S(2)}) copy-start(s32[768]{0:T(1024)} %param.12) | copy-start | bytes 9220
  17.3 7.4 %copy-start.6 = (f32[8,7,128]{2,0,1:T(8,128)S(1)}, f32[8,7,128]{2,0,1:T(8,128)}, u32[]{:S(2)}) copy-start(f32[8,7,128]{2,0,1:T(8,128)} %param.17) | copy-start | bytes 86020
  17.4 17.9 %collective-permute-start = (f32[3,64]{1,0:T(4,128)S(1)}, f32[3,64]{1,0:T(4,128)S(1)}, u32[]{:S(2)}, u32[]{:S(2)}) collective-permute-start(f32[3,64]{1,0:T(4,128)S(1)} %get-tuple-element.9), channel_id=1, source_target_pairs={{0,1},{1,2},{2,3},{3,4},{4,5},{5,6},{6,7},{7,8},{8,9},{9,10},{10,1... | collective-permute-start | bytes 2312 | tf_op jit(solution)/shard_map/ppermute | solution.py:605
  20.9 17.7 %collective-permute-start.1 = (f32[3,64]{1,0:T(4,128)S(1)}, f32[3,64]{1,0:T(4,128)S(1)}, u32[]{:S(2)}, u32[]{:S(2)}) collective-permute-start(f32[3,64]{1,0:T(4,128)S(1)} %get-tuple-element.10), channel_id=1, source_target_pairs={{1,0},{2,1},{3,2},{4,3},{5,4},{6,5},{7,6},{8,7},{9,8},{10,9},{11,1... | collective-permute-start | bytes 2312 | tf_op jit(solution)/shard_map/ppermute | solution.py:606
  23.2 21.7 %copy-start.1 = (bf16[128,128]{1,0:T(8,128)(2,1)S(1)}, bf16[128,128]{1,0:T(8,128)(2,1)}, u32[]{:S(2)}) copy-start(bf16[128,128]{1,0:T(8,128)(2,1)} %mix.1) | copy-start | bytes 98308
  23.2 21.7 %copy-start.2 = (bf16[128,128]{1,0:T(8,128)(2,1)S(1)}, bf16[128,128]{1,0:T(8,128)(2,1)}, u32[]{:S(2)}) copy-start(bf16[128,128]{1,0:T(8,128)(2,1)} %self_w.1) | copy-start | bytes 98308
  23.3 21.7 %copy-start.4 = (f32[128]{0:T(128)S(1)}, f32[128]{0:T(128)}, u32[]{:S(2)}) copy-start(f32[128]{0:T(128)} %param.21) | copy-start | bytes 1540

commit v4 on v3

--- a/solution.py
+++ b/solution.py
@@ -150,19 +150,20 @@
     )
 
 
-def message_tasks(e, low, width, edges, terms, terms0, msg):
+def message_tasks(e, low, width, edges, terms, terms0, msg, off=0):
+    part = slice(off, off + width)
     rows = pl.ds(pl.multiple_of(e * BLOCK + low, BLOCK), width)
 
     def scalar():
-        msg[0, rows, :] += mm(edges[0], terms0[:, 0:CH])
+        msg[0, rows, :] += mm(edges[0, part, :], terms0[:, 0:CH])
 
     def carried(k):
-        both = mm(edges[0], terms0[:, k * CH : (k + 2) * CH])
+        both = mm(edges[0, part, :], terms0[:, k * CH : (k + 2) * CH])
         msg[k, rows, :] += both[:, 0:CH]
         msg[k + 1, rows, :] += both[:, CH:]
 
     def paired(k):
-        both = mm(edges[k], pair_terms(terms, k))
+        both = mm(edges[k, part, :], pair_terms(terms, k))
         msg[0, rows, :] += both[:, 0:CH]
         msg[k, rows, :] += both[:, CH:]
 
@@ -173,7 +174,8 @@
     )
 
 
-def pull_tasks(e, low, width, radial, slope, terms, terms0, dmsg, by_r, by_y):
+def pull_tasks(e, low, width, radial, slope, terms, terms0, dmsg, by_r, by_y, off=0):
+    part_rows = slice(off, off + width)
     centre = pl.ds(pl.multiple_of(e * BLOCK + low, BLOCK), width)
 
     def first():
@@ -181,9 +183,9 @@
         total = None
         for m in range(4):
             sl = slice(m * CH, (m + 1) * CH)
-            part = slope[:, sl] * grad[:, sl]
+            part = slope[part_rows, sl] * grad[:, sl]
             total = part if total is None else total + part
-        by_r[0, 0:width, :] = total
+        by_r[0, part_rows, :] = total
 
     def order(k):
         lhs = jnp.concatenate([dmsg[centre, 0:CH], dmsg[centre, k * CH : (k + 1) * CH]], axis=1)
@@ -192,12 +194,12 @@
         total_y = None
         for m in range(4):
             sl = slice(m * CH, (m + 1) * CH)
-            part_r = slope[:, sl] * grad[:, sl]
-            part_y = radial[:, sl] * grad[:, sl]
+            part_r = slope[part_rows, sl] * grad[:, sl]
+            part_y = radial[part_rows, sl] * grad[:, sl]
             total_r = part_r if total_r is None else total_r + part_r
             total_y = part_y if total_y is None else total_y + part_y
-        by_r[k, 0:width, :] = total_r
-        by_y[k, 0:width, :] = total_y
+        by_r[k, part_rows, :] = total_r
+        by_y[k, part_rows, :] = total_y
 
     return [first] + [functools.partial(order, k) for k in range(1, 9)]
 
@@ -397,39 +399,54 @@
     cols[...] = jnp.zeros_like(cols)
     dmsg[...] = jnp.zeros_like(dmsg)
     last = own_blocks - 1
+    halo = ((0, 2 * BLOCK), (own_blocks + 1, 0))
     mingle(own_edges(0, edges_a), term_tasks(1, feats, weights, terms_a, first_a))
 
+    def ahead_work(b, half):
+        return own_edges(b, edge_bufs[half]) + term_tasks(
+            b + 1, feats, weights, term_bufs[half], first_bufs[half]
+        )
+
+    def message(b, half, low=0, size=width):
+        return message_tasks(
+            b + 1, low, size, edge_bufs[half], term_bufs[half], first_bufs[half], msg, low
+        )
+
+    def halo_edges(side):
+        def put_edge(k, rows, cols_, value):
+            edges_h[side, k, rows, cols_] = value
+
+        def put_slope(rows, cols_, value):
+            slopes_h[side, rows, cols_] = value
+
+        e, low = halo[side]
+        return edge_tasks(e, low, BLOCK, pos_i, pos_j, keep, put_edge, put_slope)
+
+    def halo_terms(side):
+        return term_tasks(halo[side][0], feats, weights, term_bufs[side], first_bufs[side])
+
+    def halo_message(side):
+        e, low = halo[side]
+        return message_tasks(
+            e, low, BLOCK, edges_h.at[side], term_bufs[side], first_bufs[side], msg
+        )
+
+    mingle(message(0, 0, BLOCK, 2 * BLOCK), ahead_work(1, 1))
+
     def forward(i, carry):
-        for half in range(2):
-            b = i * 2 + half
-            ahead = jnp.minimum(b + 1, last)
-            mingle(
-                message_tasks(b + 1, 0, width, edge_bufs[half], term_bufs[half], first_bufs[half], msg),
-                own_edges(ahead, edge_bufs[1 - half]),
-                term_tasks(ahead + 1, feats, weights, term_bufs[1 - half], first_bufs[1 - half]),
-            )
+        b = i * 2 + 1
+        mingle(message(b, 1), ahead_work(b + 1, 0))
+        mingle(message(b + 1, 0), ahead_work(b + 2, 1))
         return carry
 
-    lax.fori_loop(0, own_blocks // 2, forward, 0)
+    lax.fori_loop(0, own_blocks // 2 - 1, forward, 0)
+    mingle(message(last, 1, 0, 2 * BLOCK), halo_edges(0), halo_edges(1))
 
     to_before.wait()
     to_after.wait()
-    halo = ((0, 2 * BLOCK), (own_blocks + 1, 0))
-    for side, (e, low) in enumerate(halo):
-        def put_edge(k, rows, cols_, value):
-            edges_h[side, k, rows, cols_] = value
-
-        def put_slope(rows, cols_, value):
-            slopes_h[side, rows, cols_] = value
-
-        mingle(
-            edge_tasks(e, low, BLOCK, pos_i, pos_j, keep, put_edge, put_slope),
-            term_tasks(e, feats, weights, term_bufs[side], first_bufs[side]),
-        )
-    for side, (e, low) in enumerate(halo):
-        mingle(
-            message_tasks(e, low, BLOCK, edges_h.at[side], term_bufs[side], first_bufs[side], msg)
-        )
+    mingle(halo_terms(0))
+    mingle(halo_message(0), halo_terms(1))
+    mingle(halo_message(1))
 
     size = 2 * BLOCK
 
@@ -463,36 +480,44 @@
 
     lax.fori_loop(0, own_blocks // 2, atoms, 0)
 
-    for side, (e, low) in enumerate(halo):
-        mingle(
-            pull_tasks(
-                e, low, BLOCK, edges_h.at[side, 0], slopes_h.at[side], term_bufs[side],
-                first_bufs[side], dmsg, *sums_bufs[side],
-            )
-        )
-    for side, (e, low) in enumerate(halo):
-        mingle(force_tasks(e, low, BLOCK, *sums_bufs[side], pos_i, pos_j, keep, cols, nbr_out))
+    def halo_pull(side):
+        e, low = halo[side]
+        return pull_tasks(
+            e, low, BLOCK, edges_h.at[side, 0], slopes_h.at[side], term_bufs[side],
+            first_bufs[side], dmsg, *sums_bufs[side],
+        )
+
+    def halo_force(side):
+        e, low = halo[side]
+        return force_tasks(e, low, BLOCK, *sums_bufs[side], pos_i, pos_j, keep, cols, nbr_out)
+
+    mingle(halo_pull(0))
+    mingle(
+        halo_pull(1), halo_force(0), term_tasks(1, feats, weights, terms_a, first_a)
+    )
+    mingle(halo_force(1))
     force_before = send(nbr_out.at[0], inbox.at[0], 2, before)
     force_after = send(nbr_out.at[own_blocks + 1], inbox.at[1], 3, after)
     force_before.start()
     force_after.start()
-    mingle(term_tasks(1, feats, weights, terms_a, first_a))
-
-    def pull(b, half):
+
+    def pull(b, half, low=0, size=width):
         return pull_tasks(
-            b + 1, 0, width, rad_all.at[b], slope_all.at[b], term_bufs[half], first_bufs[half],
-            dmsg, *sums_bufs[half],
+            b + 1, low, size, rad_all.at[b], slope_all.at[b], term_bufs[half], first_bufs[half],
+            dmsg, *sums_bufs[half], low,
         )
 
     def ahead_terms(b, half):
         return term_tasks(b + 1, feats, weights, term_bufs[half], first_bufs[half])
 
-    def force(b, half):
+    def force(b, half, size=width):
         return force_tasks(
-            b + 1, 0, width, *sums_bufs[half], pos_i, pos_j, keep, cols, nbr_out
-        )
-
-    mingle(pull(0, 0), ahead_terms(1, 1))
+            b + 1, 0, size, *sums_bufs[half], pos_i, pos_j, keep, cols, nbr_out
+        )
+
+    for sums in sums_bufs[0]:
+        sums[:, 0:BLOCK, :] = jnp.zeros((9, BLOCK, CH), BF16)
+    mingle(pull(0, 0, BLOCK, 2 * BLOCK), ahead_terms(1, 1))
 
     def backward(i, carry):
         b = i * 2 + 1
@@ -501,8 +526,8 @@
         return carry
 
     lax.fori_loop(0, own_blocks // 2 - 1, backward, 0)
-    mingle(pull(last, 1), force(last - 1, 0))
-    mingle(force(last, 1))
+    mingle(pull(last, 1, 0, 2 * BLOCK), force(last - 1, 0))
+    mingle(force(last, 1, 2 * BLOCK))
     force_before.wait()
     force_after.wait()
     nbr_out[1] += inbox[1]

time: 96.3 us -> 94.9 us (0.985)
  Pallas kernels: 52.4 us -> 50.9 us
    pallas_call x1, Pallas kernels: 49.1 us -> 47.7 us  [block_stage(): pl.pallas_call(block_kernel, out_shape=(jax.ShapeDtypeStruct((3, own_rows...]
where the time goes in v4:
time: 94.9 us; the launch traced here: 94.6 us
  Pallas kernels  50.9 us (54%)
  waiting for transfers between devices  19.7 us (21%)
  starting transfers between devices  17.4 us (18%)
  local copies, waits for them, and re-layouts  4.12 us (4%)
    pallas_call x1, Pallas kernels, block_stage(): pl.pallas_call(block_kernel, out_shape=(jax.ShapeDtypeStruct((3, own_rows...  47.7 us
    all_to_all x1, starting transfers between devices, per_device(): lax.all_to_all(parcels, axes, split_axis=0, concat_axis=0, tiled=True)  11.9 us
    ppermute x1, waiting for transfers between devices, per_device(): low = lax.ppermute(coords[:, atom_rows - BLOCK:], axes, forward)  10.6 us
    all_to_all x1, waiting for transfers between devices, per_device(): lax.all_to_all(parcels, axes, split_axis=0, concat_axis=0, tiled=True)  5.8 us
    ppermute x1, starting transfers between devices, per_device(): low = lax.ppermute(coords[:, atom_rows - BLOCK:], axes, forward)  3.53 us
    ppermute x1, waiting for transfers between devices, per_device(): high = lax.ppermute(coords[:, :BLOCK], axes, backward)  3.34 us
    pallas_call x1, Pallas kernels, pack_stage(): pl.pallas_call(pack_kernel, out_shape=jax.ShapeDtypeStruct((rows_in.shape...  3.2 us
    unnamed x28, local copies, waits for them, and re-layouts  2.95 us
  transfers between devices with their start and end apart: 3, of which 3 were waited for; matrix products, arithmetic and copies ran while one was open for 2% of the time, Pallas kernels for 0%

profile of v4, /device:TPU:1, one launch (start us, length us, event | category | flops | bytes accessed | tf_op | source)
XLA Modules:
  0.0 94.6 jit_solution(16407524685279812507)
XLA Ops:
  0.6 0.0 copy-start
  0.6 1.5 %copy-done = bf16[768,1152]{1,0:T(8,128)(2,1)S(1)} copy-done((bf16[768,1152]{1,0:T(8,128)(2,1)S(1)}, bf16[768,1152]{1,0:T(8,128)(2,1)}, u32[]{:S(2)}) %copy-start) | copy-done | bytes 1769496
  2.1 3.2 %pack_stage.1 = bf16[1024,896]{1,0:T(8,128)(2,1)} custom-call(bf16[768,1152]{1,0:T(8,128)(2,1)S(1)} %copy-done), custom_call_target="tpu_custom_call" | custom-call | tf_op jit(solution)/shard_map/pack_stage/pallas_call | solution.py:272
  5.3 0.0 copy-start.7
  5.3 0.0 copy-start.5
  5.3 0.0 copy-start.10
  5.3 0.0 copy-start.3
  5.3 0.0 copy-start.8
  5.3 11.9 %all-to-all-start = ((bf16[128,8,896]{2,1,0:T(8,128)(2,1)}), bf16[128,8,896]{2,1,0:T(8,128)(2,1)}, u32[]{:S(2)}, u32[]{:S(2)}) async-start(bf16[128,8,896]{2,1,0:T(8,128)(2,1)} %bitcast), calls=%async_computation | async-start | bytes 3670016 | tf_op jit(solution)/shard_map/all_to_all | solution.py:626
  17.2 0.0 copy-start.9
  17.3 0.0 copy-start.6
  17.3 0.0 copy-done.7
  17.3 0.1 fusion.3
  17.4 3.5 %collective-permute-start = (f32[3,64]{1,0:T(4,128)S(1)}, f32[3,64]{1,0:T(4,128)S(1)}, u32[]{:S(2)}, u32[]{:S(2)}) collective-permute-start(f32[3,64]{1,0:T(4,128)S(1)} %get-tuple-element.9), channel_id=1, source_target_pairs={{0,1},{1,2},{2,3},{3,4},{4,5},{5,6},{6,7},{7,8},{8,9},{9,10},{10,1... | collective-permute-start | bytes 2312 | tf_op jit(solution)/shard_map/ppermute | solution.py:630
  20.9 1.9 %collective-permute-start.1 = (f32[3,64]{1,0:T(4,128)S(1)}, f32[3,64]{1,0:T(4,128)S(1)}, u32[]{:S(2)}, u32[]{:S(2)}) collective-permute-start(f32[3,64]{1,0:T(4,128)S(1)} %get-tuple-element.10), channel_id=1, source_target_pairs={{1,0},{2,1},{3,2},{4,3},{5,4},{6,5},{7,6},{8,7},{9,8},{10,9},{11,1... | collective-permute-start | bytes 2312 | tf_op jit(solution)/shard_map/ppermute | solution.py:631
  22.8 0.0 copy-done.5
  22.8 0.1 copy.28
  23.0 0.0 copy-done.10
  23.0 0.1 pad_convert_fusion
  23.1 0.1 fusion.4
  23.2 0.0 copy-done.3
  23.2 0.1 fusion.2
  23.2 0.0 copy-done.8
  23.2 0.0 copy-start.1
  23.2 0.0 copy-start.2
  23.3 0.0 copy-start.4
  23.3 0.7 fusion.gains
  24.0 0.1 copy.25
  24.1 0.1 reshape.54.keep
  24.2 0.3 reshape.61.live_in
  24.5 0.0 copy-done.9
  24.5 0.2 broadcast_in_dim.12.arrival
  24.7 0.0 copy-done.6
  24.7 10.6 %collective-permute-done = f32[3,64]{1,0:T(4,128)S(1)} collective-permute-done((f32[3,64]{1,0:T(4,128)S(1)}, f32[3,64]{1,0:T(4,128)S(1)}, u32[]{:S(2)}, u32[]{:S(2)}) %collective-permute-start) | collective-permute-done | bytes 800 | tf_op jit(solution)/shard_map/ppermute | solution.py:630
  35.3 3.3 %collective-permute-done.1 = f32[3,64]{1,0:T(4,128)S(1)} collective-permute-done((f32[3,64]{1,0:T(4,128)S(1)}, f32[3,64]{1,0:T(4,128)S(1)}, u32[]{:S(2)}, u32[]{:S(2)}) %collective-permute-start.1) | collective-permute-done | bytes 800 | tf_op jit(solution)/shard_map/ppermute | solution.py:631
  38.6 0.1 pad_maximum_fusion
  38.7 0.2 copy.26
  38.9 0.1 reshape.57
  39.0 0.1 select_maximum_fusion.pos_j
  39.1 5.8 %all-to-all-done = bf16[128,8,896]{2,1,0:T(8,128)(2,1)} async-done(((bf16[128,8,896]{2,1,0:T(8,128)(2,1)}), bf16[128,8,896]{2,1,0:T(8,128)(2,1)}, u32[]{:S(2)}, u32[]{:S(2)}) %all-to-all-start) | async-done | bytes 1835040 | tf_op jit(solution)/shard_map/all_to_all | solution.py:626
  44.9 0.0 copy-done.1
  44.9 0.0 copy-done.2
  44.9 0.0 copy-done.4
  44.9 47.7 %block_stage.1 = (f32[3,768]{1,0:T(4,128)S(1)}, f32[1,768]{1,0:T(1,128)S(1)}, bf16[768,128]{1,0:T(8,128)(2,1)S(1)}) custom-call(f32[42]{0:T(128)S(1)} %reshape.54.keep, s32[12]{0:T(128)S(1)} %copy-done.3, s32[768,1]{1,0:T(8,128)S(1)} %broadcast_in_dim.12.arrival, f32[768,1]{1,0:T(8,128)S(1)} %reshape.61.live_in, bf16[1024,896]{1,0:T(8,128)(2,1)} %bitcast.1.received, ...), custom_call_target="tpu_custom_call" | custom-call | tf_op jit(solution)/shard_map/block_stage/pallas_call | solution.py:556
  92.7 0.6 reduce
  93.3 0.6 copy.37
  93.9 0.7 copy.38
  (7 shorter events, 0.1 us)
Async XLA Ops:
  0.6 1.5 %copy-start = (bf16[768,1152]{1,0:T(8,128)(2,1)S(1)}, bf16[768,1152]{1,0:T(8,128)(2,1)}, u32[]{:S(2)}) copy-start(bf16[768,1152]{1,0:T(8,128)(2,1)} %rows_in.1) | copy-start | bytes 5308420
  5.3 12.0 %copy-start.7 = (f32[768,3]{0,1:T(4,128)S(1)}, f32[768,3]{0,1:T(4,128)}, u32[]{:S(2)}) copy-start(f32[768,3]{0,1:T(4,128)} %param.13) | copy-start | bytes 27652
  5.3 17.5 %copy-start.5 = (f32[89,3,128]{2,0,1:T(8,128)S(1)}, f32[89,3,128]{2,0,1:T(8,128)}, u32[]{:S(2)}) copy-start(f32[89,3,128]{2,0,1:T(8,128)} %param.18) | copy-start | bytes 410116
  5.3 17.7 %copy-start.10 = (s32[12,3]{0,1:T(4,128)S(1)}, s32[12,3]{0,1:T(4,128)}, u32[]{:S(2)}) copy-start(s32[12,3]{0,1:T(4,128)} %param.16) | copy-start | bytes 436
  5.3 17.9 %copy-start.3 = (s32[12]{0:T(128)S(1)}, s32[12]{0:T(128)}, u32[]{:S(2)}) copy-start(s32[12]{0:T(128)} %count.1) | copy-start | bytes 148
  5.3 17.9 %copy-start.8 = (s32[768]{0:T(1024)S(1)}, s32[768]{0:T(1024)}, u32[]{:S(2)}) copy-start(s32[768]{0:T(1024)} %param.14) | copy-start | bytes 9220
  5.3 39.6 %all-to-all-start = ((bf16[128,8,896]{2,1,0:T(8,128)(2,1)}), bf16[128,8,896]{2,1,0:T(8,128)(2,1)}, u32[]{:S(2)}, u32[]{:S(2)}) async-start(bf16[128,8,896]{2,1,0:T(8,128)(2,1)} %bitcast), calls=%async_computation | async-start | bytes 3670016 | tf_op jit(solution)/shard_map/all_to_all | solution.py:626
  17.2 7.3 %copy-start.9 = (s32[768]{0:T(1024)S(1)}, s32[768]{0:T(1024)}, u32[]{:S(2)}) copy-start(s32[768]{0:T(1024)} %param.12) | copy-start | bytes 9220
  17.3 7.4 %copy-start.6 = (f32[8,7,128]{2,0,1:T(8,128)S(1)}, f32[8,7,128]{2,0,1:T(8,128)}, u32[]{:S(2)}) copy-start(f32[8,7,128]{2,0,1:T(8,128)} %param.17) | copy-start | bytes 86020
  17.4 17.9 %collective-permute-start = (f32[3,64]{1,0:T(4,128)S(1)}, f32[3,64]{1,0:T(4,128)S(1)}, u32[]{:S(2)}, u32[]{:S(2)}) collective-permute-start(f32[3,64]{1,0:T(4,128)S(1)} %get-tuple-element.9), channel_id=1, source_target_pairs={{0,1},{1,2},{2,3},{3,4},{4,5},{5,6},{6,7},{7,8},{8,9},{9,10},{10,1... | collective-permute-start | bytes 2312 | tf_op jit(solution)/shard_map/ppermute | solution.py:630
  20.9 17.7 %collective-permute-start.1 = (f32[3,64]{1,0:T(4,128)S(1)}, f32[3,64]{1,0:T(4,128)S(1)}, u32[]{:S(2)}, u32[]{:S(2)}) collective-permute-start(f32[3,64]{1,0:T(4,128)S(1)} %get-tuple-element.10), channel_id=1, source_target_pairs={{1,0},{2,1},{3,2},{4,3},{5,4},{6,5},{7,6},{8,7},{9,8},{10,9},{11,1... | collective-permute-start | bytes 2312 | tf_op jit(solution)/shard_map/ppermute | solution.py:631
  23.2 21.7 %copy-start.1 = (bf16[128,128]{1,0:T(8,128)(2,1)S(1)}, bf16[128,128]{1,0:T(8,128)(2,1)}, u32[]{:S(2)}) copy-start(bf16[128,128]{1,0:T(8,128)(2,1)} %mix.1) | copy-start | bytes 98308
  23.2 21.7 %copy-start.2 = (bf16[128,128]{1,0:T(8,128)(2,1)S(1)}, bf16[128,128]{1,0:T(8,128)(2,1)}, u32[]{:S(2)}) copy-start(bf16[128,128]{1,0:T(8,128)(2,1)} %self_w.1) | copy-start | bytes 98308
  23.3 21.7 %copy-start.4 = (f32[128]{0:T(128)S(1)}, f32[128]{0:T(128)}, u32[]{:S(2)}) copy-start(f32[128]{0:T(128)} %param.21) | copy-start | bytes 1540

commit v5 on v4

--- a/solution.py
+++ b/solution.py
@@ -254,17 +254,24 @@
     parcel, within = row // 8, row % 8
     plain = ((within < PIECE) & (col == parcel * PIECE + within)).astype(F32).astype(BF16)
     last = lax.broadcasted_iota(jnp.int32, (group, CH), 0) % 8 == PIECE + 1
-    for t in range(7):
-        cols = slice(t * CH, (t + 1) * CH)
-        if t < PIECE:
-            extra = ((within >= PIECE) & (col == parcel * PIECE + t)).astype(F32).astype(BF16)
+    for pair in range(0, 7, 2):
+        tiles = range(pair, min(pair + 2, 7))
+        extras = [
+            ((within >= PIECE) & (col == parcel * PIECE + t)).astype(F32).astype(BF16)
+            for t in tiles
+            if t < PIECE
+        ]
         for g in range(out.shape[0] // group):
             at = slice(g * source, (g + 1) * source)
-            value = mm(plain, rows_in[at, cols])
-            if t < PIECE:
+            value = mm(plain, rows_in[at, pair * CH : (pair + len(tiles)) * CH])
+            for step, extra in enumerate(extras):
                 both = mm(extra, rows_in[at, 7 * CH : 9 * CH])
-                value += jnp.where(last, both[:, CH:], both[:, 0:CH])
-            out[g * group : (g + 1) * group, cols] = value.astype(BF16)
+                cols = slice((pair + step) * CH, (pair + step + 1) * CH)
+                part = value[:, step * CH : (step + 1) * CH]
+                part += jnp.where(last, both[:, CH:], both[:, 0:CH])
+                out[g * group : (g + 1) * group, cols] = part.astype(BF16)
+            if not extras:
+                out[g * group : (g + 1) * group, pair * CH : (pair + 1) * CH] = value.astype(BF16)
 
 
 def pack_stage(rows_in):

time: 94.9 us -> 94.5 us (level)
  no operation moved by 1% of the time
where the time goes in v5:
time: 94.5 us; the launch traced here: 94.2 us
  Pallas kernels  50.6 us (54%)
  waiting for transfers between devices  19.7 us (21%)
  starting transfers between devices  17.4 us (18%)
  local copies, waits for them, and re-layouts  4.12 us (4%)
    pallas_call x1, Pallas kernels, block_stage(): pl.pallas_call(block_kernel, out_shape=(jax.ShapeDtypeStruct((3, own_rows...  47.8 us
    all_to_all x1, starting transfers between devices, per_device(): lax.all_to_all(parcels, axes, split_axis=0, concat_axis=0, tiled=True)  11.9 us
    ppermute x1, waiting for transfers between devices, per_device(): low = lax.ppermute(coords[:, atom_rows - BLOCK:], axes, forward)  10.6 us
    all_to_all x1, waiting for transfers between devices, per_device(): lax.all_to_all(parcels, axes, split_axis=0, concat_axis=0, tiled=True)  5.8 us
    ppermute x1, starting transfers between devices, per_device(): low = lax.ppermute(coords[:, atom_rows - BLOCK:], axes, forward)  3.53 us
    ppermute x1, waiting for transfers between devices, per_device(): high = lax.ppermute(coords[:, :BLOCK], axes, backward)  3.34 us
    unnamed x28, local copies, waits for them, and re-layouts  2.95 us
    pallas_call x1, Pallas kernels, pack_stage(): pl.pallas_call(pack_kernel, out_shape=jax.ShapeDtypeStruct((rows_in.shape...  2.81 us
  transfers between devices with their start and end apart: 3, of which 3 were waited for; matrix products, arithmetic and copies ran while one was open for 2% of the time, Pallas kernels for 0%

profile of v5, /device:TPU:1, one launch (start us, length us, event | category | flops | bytes accessed | tf_op | source)
XLA Modules:
  0.0 94.2 jit_solution(13279212758760493006)
XLA Ops:
  0.6 0.0 copy-start
  0.6 1.5 %copy-done = bf16[768,1152]{1,0:T(8,128)(2,1)S(1)} copy-done((bf16[768,1152]{1,0:T(8,128)(2,1)S(1)}, bf16[768,1152]{1,0:T(8,128)(2,1)}, u32[]{:S(2)}) %copy-start) | copy-done | bytes 1769496
  2.1 2.8 %pack_stage.1 = bf16[1024,896]{1,0:T(8,128)(2,1)} custom-call(bf16[768,1152]{1,0:T(8,128)(2,1)S(1)} %copy-done), custom_call_target="tpu_custom_call" | custom-call | tf_op jit(solution)/shard_map/pack_stage/pallas_call | solution.py:279
  4.9 0.0 copy-start.7
  4.9 0.0 copy-start.5
  4.9 0.0 copy-start.10
  4.9 0.0 copy-start.3
  4.9 0.0 copy-start.8
  4.9 11.9 %all-to-all-start = ((bf16[128,8,896]{2,1,0:T(8,128)(2,1)}), bf16[128,8,896]{2,1,0:T(8,128)(2,1)}, u32[]{:S(2)}, u32[]{:S(2)}) async-start(bf16[128,8,896]{2,1,0:T(8,128)(2,1)} %bitcast), calls=%async_computation | async-start | bytes 3670016 | tf_op jit(solution)/shard_map/all_to_all | solution.py:633
  16.9 0.0 copy-start.9
  16.9 0.0 copy-start.6
  16.9 0.0 copy-done.7
  16.9 0.1 fusion.3
  17.0 3.5 %collective-permute-start = (f32[3,64]{1,0:T(4,128)S(1)}, f32[3,64]{1,0:T(4,128)S(1)}, u32[]{:S(2)}, u32[]{:S(2)}) collective-permute-start(f32[3,64]{1,0:T(4,128)S(1)} %get-tuple-element.9), channel_id=1, source_target_pairs={{0,1},{1,2},{2,3},{3,4},{4,5},{5,6},{6,7},{7,8},{8,9},{9,10},{10,1... | collective-permute-start | bytes 2312 | tf_op jit(solution)/shard_map/ppermute | solution.py:637
  20.5 1.9 %collective-permute-start.1 = (f32[3,64]{1,0:T(4,128)S(1)}, f32[3,64]{1,0:T(4,128)S(1)}, u32[]{:S(2)}, u32[]{:S(2)}) collective-permute-start(f32[3,64]{1,0:T(4,128)S(1)} %get-tuple-element.10), channel_id=1, source_target_pairs={{1,0},{2,1},{3,2},{4,3},{5,4},{6,5},{7,6},{8,7},{9,8},{10,9},{11,1... | collective-permute-start | bytes 2312 | tf_op jit(solution)/shard_map/ppermute | solution.py:638
  22.4 0.0 copy-done.5
  22.4 0.1 copy.28
  22.6 0.0 copy-done.10
  22.6 0.1 pad_convert_fusion
  22.7 0.1 fusion.4
  22.8 0.0 copy-done.3
  22.8 0.1 fusion.2
  22.9 0.0 copy-done.8
  22.9 0.0 copy-start.1
  22.9 0.0 copy-start.2
  22.9 0.0 copy-start.4
  22.9 0.7 fusion.gains
  23.6 0.1 copy.25
  23.7 0.1 reshape.54.keep
  23.8 0.3 reshape.61.live_in
  24.1 0.0 copy-done.9
  24.1 0.2 broadcast_in_dim.12.arrival
  24.3 0.0 copy-done.6
  24.3 10.6 %collective-permute-done = f32[3,64]{1,0:T(4,128)S(1)} collective-permute-done((f32[3,64]{1,0:T(4,128)S(1)}, f32[3,64]{1,0:T(4,128)S(1)}, u32[]{:S(2)}, u32[]{:S(2)}) %collective-permute-start) | collective-permute-done | bytes 800 | tf_op jit(solution)/shard_map/ppermute | solution.py:637
  34.9 3.3 %collective-permute-done.1 = f32[3,64]{1,0:T(4,128)S(1)} collective-permute-done((f32[3,64]{1,0:T(4,128)S(1)}, f32[3,64]{1,0:T(4,128)S(1)}, u32[]{:S(2)}, u32[]{:S(2)}) %collective-permute-start.1) | collective-permute-done | bytes 800 | tf_op jit(solution)/shard_map/ppermute | solution.py:638
  38.2 0.1 pad_maximum_fusion
  38.3 0.2 copy.26
  38.5 0.1 reshape.57
  38.6 0.1 select_maximum_fusion.pos_j
  38.7 5.8 %all-to-all-done = bf16[128,8,896]{2,1,0:T(8,128)(2,1)} async-done(((bf16[128,8,896]{2,1,0:T(8,128)(2,1)}), bf16[128,8,896]{2,1,0:T(8,128)(2,1)}, u32[]{:S(2)}, u32[]{:S(2)}) %all-to-all-start) | async-done | bytes 1835040 | tf_op jit(solution)/shard_map/all_to_all | solution.py:633
  44.5 0.0 copy-done.1
  44.5 0.0 copy-done.2
  44.5 0.0 copy-done.4
  44.6 47.8 %block_stage.1 = (f32[3,768]{1,0:T(4,128)S(1)}, f32[1,768]{1,0:T(1,128)S(1)}, bf16[768,128]{1,0:T(8,128)(2,1)S(1)}) custom-call(f32[42]{0:T(128)S(1)} %reshape.54.keep, s32[12]{0:T(128)S(1)} %copy-done.3, s32[768,1]{1,0:T(8,128)S(1)} %broadcast_in_dim.12.arrival, f32[768,1]{1,0:T(8,128)S(1)} %reshape.61.live_in, bf16[1024,896]{1,0:T(8,128)(2,1)} %bitcast.1.received, ...), custom_call_target="tpu_custom_call" | custom-call | tf_op jit(solution)/shard_map/block_stage/pallas_call | solution.py:563
  92.3 0.6 reduce
  92.9 0.6 copy.37
  93.5 0.7 copy.38
  (7 shorter events, 0.1 us)
Async XLA Ops:
  0.6 1.5 %copy-start = (bf16[768,1152]{1,0:T(8,128)(2,1)S(1)}, bf16[768,1152]{1,0:T(8,128)(2,1)}, u32[]{:S(2)}) copy-start(bf16[768,1152]{1,0:T(8,128)(2,1)} %rows_in.1) | copy-start | bytes 5308420
  4.9 12.0 %copy-start.7 = (f32[768,3]{0,1:T(4,128)S(1)}, f32[768,3]{0,1:T(4,128)}, u32[]{:S(2)}) copy-start(f32[768,3]{0,1:T(4,128)} %param.13) | copy-start | bytes 27652
  4.9 17.5 %copy-start.5 = (f32[89,3,128]{2,0,1:T(8,128)S(1)}, f32[89,3,128]{2,0,1:T(8,128)}, u32[]{:S(2)}) copy-start(f32[89,3,128]{2,0,1:T(8,128)} %param.18) | copy-start | bytes 410116
  4.9 17.7 %copy-start.10 = (s32[12,3]{0,1:T(4,128)S(1)}, s32[12,3]{0,1:T(4,128)}, u32[]{:S(2)}) copy-start(s32[12,3]{0,1:T(4,128)} %param.16) | copy-start | bytes 436
  4.9 17.9 %copy-start.3 = (s32[12]{0:T(128)S(1)}, s32[12]{0:T(128)}, u32[]{:S(2)}) copy-start(s32[12]{0:T(128)} %count.1) | copy-start | bytes 148
  4.9 17.9 %copy-start.8 = (s32[768]{0:T(1024)S(1)}, s32[768]{0:T(1024)}, u32[]{:S(2)}) copy-start(s32[768]{0:T(1024)} %param.14) | copy-start | bytes 9220
  4.9 39.6 %all-to-all-start = ((bf16[128,8,896]{2,1,0:T(8,128)(2,1)}), bf16[128,8,896]{2,1,0:T(8,128)(2,1)}, u32[]{:S(2)}, u32[]{:S(2)}) async-start(bf16[128,8,896]{2,1,0:T(8,128)(2,1)} %bitcast), calls=%async_computation | async-start | bytes 3670016 | tf_op jit(solution)/shard_map/all_to_all | solution.py:633
  16.9 7.3 %copy-start.9 = (s32[768]{0:T(1024)S(1)}, s32[768]{0:T(1024)}, u32[]{:S(2)}) copy-start(s32[768]{0:T(1024)} %param.12) | copy-start | bytes 9220
  16.9 7.4 %copy-start.6 = (f32[8,7,128]{2,0,1:T(8,128)S(1)}, f32[8,7,128]{2,0,1:T(8,128)}, u32[]{:S(2)}) copy-start(f32[8,7,128]{2,0,1:T(8,128)} %param.17) | copy-start | bytes 86020
  17.0 17.9 %collective-permute-start = (f32[3,64]{1,0:T(4,128)S(1)}, f32[3,64]{1,0:T(4,128)S(1)}, u32[]{:S(2)}, u32[]{:S(2)}) collective-permute-start(f32[3,64]{1,0:T(4,128)S(1)} %get-tuple-element.9), channel_id=1, source_target_pairs={{0,1},{1,2},{2,3},{3,4},{4,5},{5,6},{6,7},{7,8},{8,9},{9,10},{10,1... | collective-permute-start | bytes 2312 | tf_op jit(solution)/shard_map/ppermute | solution.py:637
  20.5 17.7 %collective-permute-start.1 = (f32[3,64]{1,0:T(4,128)S(1)}, f32[3,64]{1,0:T(4,128)S(1)}, u32[]{:S(2)}, u32[]{:S(2)}) collective-permute-start(f32[3,64]{1,0:T(4,128)S(1)} %get-tuple-element.10), channel_id=1, source_target_pairs={{1,0},{2,1},{3,2},{4,3},{5,4},{6,5},{7,6},{8,7},{9,8},{10,9},{11,1... | collective-permute-start | bytes 2312 | tf_op jit(solution)/shard_map/ppermute | solution.py:638
  22.9 21.7 %copy-start.1 = (bf16[128,128]{1,0:T(8,128)(2,1)S(1)}, bf16[128,128]{1,0:T(8,128)(2,1)}, u32[]{:S(2)}) copy-start(bf16[128,128]{1,0:T(8,128)(2,1)} %mix.1) | copy-start | bytes 98308
  22.9 21.7 %copy-start.2 = (bf16[128,128]{1,0:T(8,128)(2,1)S(1)}, bf16[128,128]{1,0:T(8,128)(2,1)}, u32[]{:S(2)}) copy-start(bf16[128,128]{1,0:T(8,128)(2,1)} %self_w.1) | copy-start | bytes 98308
  22.9 21.7 %copy-start.4 = (f32[128]{0:T(128)S(1)}, f32[128]{0:T(128)}, u32[]{:S(2)}) copy-start(f32[128]{0:T(128)} %param.21) | copy-start | bytes 1540
